TPU v7x, 128 devices: a whole 4x4x4 slice. The times are simulated.
128 devices in a mesh: sec: 4 (over y_hi, core), dev: 32 (over z, y_lo, x).
Axes of the slice: x: 4, y: 4 (y_hi: 2, y_lo: 2; y = y_hi * 2 + y_lo), z: 4, core: 2. Of those that a mesh axis runs over, the one named last changes fastest.
Arguments:
- queries: bfloat16 [256, 8192], P('dev', 'sec')
- fresh_key_value: bfloat16 [2, 256, 512], P(None, 'dev', 'sec'), may hold values from -6 to 6
- key_value_cache: bfloat16 [2, 256, 1024, 512], P(None, 'dev', None, 'sec'), may hold values from -6 to 6
- lengths: int32 [256], P('dev'), may hold values from 1 to 1024, as said below
- residual: bfloat16 [256, 4096], P(None, 'dev'), may hold values from -6 to 6
- out_weight: bfloat16 [8192, 4096], P('sec', 'dev'), may hold values from -0.0625 to 0.0625
- norm_gain: float32 [4096], P('dev'), may hold values from 0.1 to 1.9
- routes: int32 [256, 8], replicated, may hold values from 0 to 63, all different within a row; in each aligned block of 256 rows (0 to 255, 256 to 511, ...) at most 64 rows name the same one
- route_weights: float32 [256, 8], replicated, may hold values from 0.05 to 0.5
- w_gate: bfloat16 [64, 4096, 1536], P('dev', None, 'sec'), may hold values from -0.09375 to 0.09375
- w_up: bfloat16 [64, 4096, 1536], P('dev', None, 'sec'), may hold values from -0.09375 to 0.09375
- w_down: bfloat16 [64, 1536, 4096], P('dev', 'sec'), may hold values from -0.15625 to 0.15625
Outputs:
- layer_out: bfloat16 [256, 4096], P(None, 'dev')
Inputs may be any that keep to these rules, and one draw needn't show every extreme that they name: `routes`: each row names 8 different experts; no expert is named by more than 64 rows, a bound that some block reaches. `lengths`: some row has all 1024 slots filled.
All inputs are finite; a program needn't handle non-finite values.
Results may differ from a plain program's by a relative error of at most 0.0055.
Values may be sent and summed in bfloat16 or wider, within the bound.
No kernel may reach another device: no remote copies, remote signals or barrier semaphores. Data moves between devices by JAX's collectives and lax.ppermute only.
A program may use at most 128 MiB of HBM per device.

v0:
```python
import math

import jax
import jax.numpy as jnp
from jax import lax
from jax.sharding import PartitionSpec as P

D = 4096
QUERY_HEADS = 64
KEY_VALUE_HEADS = 4
HEAD_SIZE = 128
CAP = 64


def attend(queries, fresh_key_value, key_value_cache, lengths):
    row_count = key_value_cache.shape[1]
    cache_length = key_value_cache.shape[2]
    heads_kv = key_value_cache.shape[3] // HEAD_SIZE
    queries_per_group = QUERY_HEADS // KEY_VALUE_HEADS
    score_scale = 1.0 / math.sqrt(HEAD_SIZE)
    head_queries = queries.reshape(row_count, heads_kv, queries_per_group, HEAD_SIZE)
    cached_keys = key_value_cache[0].reshape(row_count, cache_length, heads_kv, HEAD_SIZE)
    cached_values = key_value_cache[1].reshape(row_count, cache_length, heads_kv, HEAD_SIZE)
    own_key = fresh_key_value[0].reshape(row_count, heads_kv, HEAD_SIZE)
    own_value = fresh_key_value[1].reshape(row_count, heads_kv, HEAD_SIZE).astype(jnp.float32)
    scores = (
        jnp.einsum("rkgd,rtkd->rkgt", head_queries, cached_keys, preferred_element_type=jnp.float32)
        * score_scale
    )
    own_score = (
        jnp.einsum("rkgd,rkd->rkg", head_queries, own_key, preferred_element_type=jnp.float32)
        * score_scale
    )
    visible = (jnp.arange(cache_length, dtype=jnp.int32)[None, :] < lengths[:, None])[
        :, None, None, :
    ]
    row_max = jnp.maximum(jnp.max(jnp.where(visible, scores, -jnp.inf), axis=-1), own_score)
    weights = jnp.where(visible, jnp.exp(scores - row_max[..., None]), 0.0)
    own_weight = jnp.exp(own_score - row_max)
    normalizer = jnp.sum(weights, axis=-1) + own_weight
    weighted = jnp.einsum(
        "rkgt,rtkd->rkgd",
        weights.astype(jnp.bfloat16),
        cached_values,
        preferred_element_type=jnp.float32,
    )
    weighted = weighted + own_weight[..., None] * own_value[:, :, None, :]
    return (
        (weighted / normalizer[..., None])
        .astype(jnp.bfloat16)
        .reshape(row_count, heads_kv * queries_per_group * HEAD_SIZE)
    )


def slot_layout(routes, route_weights, expert_ids):
    matches = routes[:, :, None] == expert_ids[None, None, :]
    chosen = jnp.any(matches, axis=1)
    shares = jnp.sum(jnp.where(matches, route_weights[:, :, None], 0.0), axis=1)
    slot_rank = jnp.cumsum(chosen.astype(jnp.int32), axis=0, dtype=jnp.int32) - 1
    slot_ids = jnp.arange(CAP, dtype=jnp.int32)
    slot_mask = (chosen[:, :, None] & (slot_rank[:, :, None] == slot_ids[None, None, :])).transpose(
        1, 2, 0
    )
    spread = slot_mask.astype(jnp.float32) * shares.T[:, None, :]
    return (slot_mask, spread)


def expert_results(full_rows, slot_mask, w_gate, w_up, w_down):
    picked = jnp.einsum(
        "ecr,rd->ecd", slot_mask.astype(jnp.bfloat16), full_rows, preferred_element_type=jnp.float32
    ).astype(jnp.bfloat16)
    gate_part = jnp.einsum("ecd,edf->ecf", picked, w_gate, preferred_element_type=jnp.float32)
    upward = jnp.einsum("ecd,edf->ecf", picked, w_up, preferred_element_type=jnp.float32)
    activation = (jax.nn.silu(gate_part) * upward).astype(jnp.bfloat16)
    return jnp.einsum("ecf,efd->ecd", activation, w_down, preferred_element_type=jnp.float32)


def shards(
    queries,
    fresh_key_value,
    key_value_cache,
    lengths,
    residual,
    out_weight,
    norm_gain,
    routes,
    route_weights,
    w_gate,
    w_up,
    w_down,
):
    attn = attend(queries, fresh_key_value, key_value_cache, lengths)
    partial_out = jnp.dot(
        lax.all_gather(attn, "dev", axis=0, tiled=True),
        out_weight,
        preferred_element_type=jnp.float32,
    )
    hidden = residual.astype(jnp.float32) + lax.psum(partial_out, "sec")
    square_sum = lax.psum(jnp.sum(hidden * hidden, axis=-1, keepdims=True), "dev")
    normed = (hidden * lax.rsqrt(square_sum / D + 1e-06) * norm_gain).astype(jnp.bfloat16)
    full_rows = lax.all_gather(normed, "dev", axis=1, tiled=True)
    local_count = w_gate.shape[0]
    local_ids = lax.axis_index("dev") * local_count + jnp.arange(local_count, dtype=jnp.int32)
    slot_mask, spread = slot_layout(routes, route_weights, local_ids)
    result = expert_results(full_rows, slot_mask, w_gate, w_up, w_down)
    expert_term = jnp.einsum("ecr,ecd->rd", spread, result, precision=lax.Precision.HIGHEST)
    mixture = lax.psum(lax.psum_scatter(expert_term, "dev", scatter_dimension=1, tiled=True), "sec")
    return (hidden + mixture).astype(jnp.bfloat16)


def solution(mesh):
    return jax.shard_map(
        shards,
        mesh=mesh,
        in_specs=(
            P("dev", "sec"),
            P(None, "dev", "sec"),
            P(None, "dev", None, "sec"),
            P("dev"),
            P(None, "dev"),
            P("sec", "dev"),
            P("dev"),
            P(),
            P(),
            P("dev", None, "sec"),
            P("dev", None, "sec"),
            P("dev", "sec", None),
        ),
        out_specs=P(None, "dev"),
        check_vma=False,
    )
```

profile of v0, /device:TPU:0, one launch (start us, length us, event | category | flops | bytes accessed | tf_op | source)
XLA Modules:
  0.0 651.8 jit_solution(15178874167412993256)
XLA Ops:
  6.5 0.8 bitcast_convert_fusion
  7.3 0.7 iota_compare_fusion.1
  8.0 0.9 fusion.46
  8.9 2.4 select_reduce_fusion
  11.3 0.2 fusion.24
  11.6 2.1 fusion.21
  13.7 0.6 copy.34
  14.4 153.6 %all-gather.3.cloned.1.call-done = bf16[256,2048]{1,0:T(8,128)(2,1)} async-done(((bf16[8,2048]{1,0:T(8,128)(2,1)}), bf16[256,2048]{1,0:T(8,128)(2,1)}) %all-gather.3.cloned.1.call-update) | async-done | bytes 1048592 | tf_op jit(solution)/shard_map/all_gather | solution.py:94
  168.0 2.3 fusion.55
  170.4 40.2 %all-reduce.3.cloned.1.call-done = f32[256,128]{1,0:T(8,128)} async-done(((f32[256,128]{1,0:T(8,128)}), f32[256,128]{1,0:T(8,128)}) %all-reduce.3.cloned.1.call-update) | async-done | bytes 131088 | tf_op jit(solution)/shard_map/psum | solution.py:98
  210.6 1.0 multiply_reduce_fusion
  211.6 81.9 %psum.22 = f32[256,1]{0,1:T(1,128)S(1)} all-reduce(f32[256,1]{0,1:T(1,128)S(1)} %bitcast.67), channel_id=1, replica_groups=mesh['sec'=4,'dev'=32] {'dev'}, use_global_device_ids=true, to_apply=%region_8.9 | all-reduce | flops 256 | bytes 2048 | tf_op jit(solution)/shard_map/psum | solution.py:99
  293.5 1.6 multiply_convert_fusion
  295.4 0.6 reduce-window.6
  296.0 0.2 slice_reduce_fusion
  296.2 0.2 reduce-window.9
  296.6 119.3 %all-gather.5.cloned.1.call-done = bf16[256,4096]{1,0:T(8,128)(2,1)} async-done(((bf16[256,128]{1,0:T(8,128)(2,1)}), bf16[256,4096]{1,0:T(8,128)(2,1)}) %all-gather.5.cloned.1.call-update) | async-done | bytes 2097168 | tf_op jit(solution)/shard_map/all_gather | solution.py:101
  415.9 2.0 convolution_convert_fusion
  417.9 3.8 fusion.56
  421.8 8.1 %fusion.11 = f32[2,64,4096]{2,1,0:T(8,128)} fusion(bf16[2,384,4096]{2,1,0:T(8,128)(2,1)} %param.23, bf16[2,64,4096]{2,1,0:T(8,128)(2,1)S(1)} %convolution_convert_fusion, bf16[2,4096,384]{2,1,0:T(8,128)(2,1)} %param.22, f32[2,64,384]{2,1,0:T(8,128)S(1)} %fusion.56), kind=kOutput, calls=%fused_computation.12 | convolution fusion | flops 805601280 | bytes 15925248 | tf_op jit(solution)/shard_map/ecf,efd->ecd/dot_general | solution.py:75
  429.9 6.8 %convolution_bitcast_fusion = f32[256,4096]{1,0:T(8,128)} fusion(f32[2,64,4096]{2,1,0:T(8,128)} %fusion.11, f32[2,256]{1,0:T(2,128)S(1)} %bitcast.65, s32[2,256]{1,0:T(2,128)S(1)} %bitcast.58, pred[2,256]{1,0:T(4,128)(4,1)S(1)} %bitcast.62), kind=kOutput, calls=%fused_computation | convolution fusion | flops 1610711040 | bytes 6296064 | tf_op jit(solution)/shard_map/ecr,ecd->rd/dot_general | solution.py:106
  436.7 168.4 %reduce-scatter.2.cloned.1.call-done = f32[256,128]{1,0:T(8,128)} async-done(((f32[256,4096]{1,0:T(8,128)}), f32[256,128]{1,0:T(8,128)}) %reduce-scatter.2.cloned.1.call-update) | async-done | bytes 131088 | tf_op jit(solution)/shard_map/reduce_scatter | solution.py:107
  605.1 38.6 %all-reduce.5.cloned.1.call-done = f32[256,128]{1,0:T(8,128)} async-done(((f32[256,128]{1,0:T(8,128)}), f32[256,128]{1,0:T(8,128)}) %all-reduce.5.cloned.1.call-update) | async-done | bytes 131088 | tf_op jit(solution)/shard_map/psum | solution.py:107
  643.7 1.6 add_convert_fusion
  (32 shorter events, 0.6 us)
Async XLA Ops:
  6.5 161.5 %copy-start = (bf16[2048,128]{1,0:T(8,128)(2,1)S(1)}, bf16[2048,128]{1,0:T(8,128)(2,1)}, u32[]{:S(2)}) copy-start(bf16[2048,128]{1,0:T(8,128)(2,1)} %param.17) | copy-start | bytes 1572868
  6.5 204.1 %copy-start.2 = (bf16[256,128]{1,0:T(8,128)(2,1)S(1)}, bf16[256,128]{1,0:T(8,128)(2,1)}, u32[]{:S(2)}) copy-start(bf16[256,128]{1,0:T(8,128)(2,1)} %param.16) | copy-start | bytes 196612
  6.5 161.5 %all-gather.3.cloned.1.call-start = ((), (), s32[]{:S(2)}) async-start(), calls=%async_computation.1 | async-start | bytes 1081344 | tf_op jit(solution)/shard_map/all_gather | solution.py:94
  8.9 284.6 %copy-start.5 = (f32[128]{0:T(128)S(1)}, f32[128]{0:T(128)}, u32[]{:S(2)}) copy-start(f32[128]{0:T(128)} %param.18) | copy-start | bytes 1540
  8.9 286.3 %copy-start.3 = (s32[256,8]{0,1:T(8,128)S(1)}, s32[256,8]{0,1:T(8,128)}, u32[]{:S(2)}) copy-start(s32[256,8]{0,1:T(8,128)} %param.19) | copy-start | bytes 24580
  8.9 287.6 %copy-start.4 = (f32[256,8]{0,1:T(8,128)S(1)}, f32[256,8]{0,1:T(8,128)}, u32[]{:S(2)}) copy-start(f32[256,8]{0,1:T(8,128)} %param.20) | copy-start | bytes 24580
  14.3 196.3 %all-reduce.3.cloned.1.call-start = ((), (), s32[]{:S(2)}) async-start(), calls=%async_computation.2 | async-start | bytes 262144 | tf_op jit(solution)/shard_map/psum | solution.py:98
  170.3 245.6 %all-gather.5.cloned.1.call-start = ((), (), s32[]{:S(2)}) async-start(), calls=%async_computation.3 | async-start | bytes 2162688 | tf_op jit(solution)/shard_map/all_gather | solution.py:101
  295.2 309.9 %reduce-scatter.2.cloned.1.call-start = ((), (), s32[]{:S(2)}) async-start(), calls=%async_computation.4 | async-start | bytes 4325376 | tf_op jit(solution)/shard_map/reduce_scatter | solution.py:107
  429.9 213.9 %copy-start.1 = (f32[256,128]{1,0:T(8,128)S(1)}, f32[256,128]{1,0:T(8,128)}, u32[]{:S(2)}) copy-start(f32[256,128]{1,0:T(8,128)} %all-reduce.3.cloned.1.call-done) | copy-start | bytes 393220
  436.6 207.1 %all-reduce.5.cloned.1.call-start = ((), (), s32[]{:S(2)}) async-start(), calls=%async_computation.5 | async-start | bytes 262144 | tf_op jit(solution)/shard_map/psum | solution.py:107
Sparse Core Ops, SparseCore 0:
  14.4 153.5 all-gather.2
  170.5 40.0 all-reduce.2
  295.3 120.5 all-gather.4
  436.8 168.2 reduce-scatter.1
  607.5 36.1 all-reduce.4
where the time goes:
time: 654 us; the launch traced here: 652 us
  waiting for transfers between devices  520 us (80%)
  blocking collectives  81.9 us (13%)
  matrix products  28.3 us (4%)
  between operations  13.2 us (2%)
  other arithmetic  7.04 us (1%)
    reduce_scatter x1, waiting for transfers between devices, shards(): lax.psum_scatter(expert_term, 'dev', scatter_dimension=1, tiled=True)  168 us
    all_gather x1, waiting for transfers between devices, shards(): lax.all_gather(attn, 'dev', axis=0, tiled=True)  154 us
    all_gather x1, waiting for transfers between devices, shards(): full_rows = lax.all_gather(normed, 'dev', axis=1, tiled=True)  119 us
    psum x1, blocking collectives, shards(): lax.psum(jnp.sum(hidden * hidden, axis=-1, keepdims=True), 'dev')  81.9 us
    psum x1, waiting for transfers between devices, shards(): hidden = residual.astype(jnp.float32) + lax.psum(partial_out, 'sec')  40.2 us
    psum x1, waiting for transfers between devices, shards(): lax.psum(lax.psum_scatter(expert_term, 'dev', scatter_dimension=1, tiled=...  38.6 us
  transfers between devices with their start and end apart: 5, of which 5 were waited for; matrix products, arithmetic and copies ran while one was open for 0% of the time, Pallas kernels for 0%

commit v1 on v0

--- a/solution.py
+++ b/solution.py
@@ -10,6 +10,8 @@
 KEY_VALUE_HEADS = 4
 HEAD_SIZE = 128
 CAP = 64
+GROUPS = 32
+CORE_SWAP = [(0, 1), (1, 0), (2, 3), (3, 2)]
 
 
 def attend(queries, fresh_key_value, key_value_cache, lengths):
@@ -52,27 +54,29 @@
     )
 
 
-def slot_layout(routes, route_weights, expert_ids):
-    matches = routes[:, :, None] == expert_ids[None, None, :]
-    chosen = jnp.any(matches, axis=1)
-    shares = jnp.sum(jnp.where(matches, route_weights[:, :, None], 0.0), axis=1)
-    slot_rank = jnp.cumsum(chosen.astype(jnp.int32), axis=0, dtype=jnp.int32) - 1
-    slot_ids = jnp.arange(CAP, dtype=jnp.int32)
-    slot_mask = (chosen[:, :, None] & (slot_rank[:, :, None] == slot_ids[None, None, :])).transpose(
-        1, 2, 0
-    )
-    spread = slot_mask.astype(jnp.float32) * shares.T[:, None, :]
-    return (slot_mask, spread)
+def three_terms(values):
+    high = lax.reduce_precision(values, 8, 7)
+    rest = values - high
+    middle = lax.reduce_precision(rest, 8, 7)
+    low = rest - middle
+    return jnp.stack([high, middle, low]).astype(jnp.bfloat16)
 
 
-def expert_results(full_rows, slot_mask, w_gate, w_up, w_down):
-    picked = jnp.einsum(
-        "ecr,rd->ecd", slot_mask.astype(jnp.bfloat16), full_rows, preferred_element_type=jnp.float32
-    ).astype(jnp.bfloat16)
-    gate_part = jnp.einsum("ecd,edf->ecf", picked, w_gate, preferred_element_type=jnp.float32)
-    upward = jnp.einsum("ecd,edf->ecf", picked, w_up, preferred_element_type=jnp.float32)
-    activation = (jax.nn.silu(gate_part) * upward).astype(jnp.bfloat16)
-    return jnp.einsum("ecf,efd->ecd", activation, w_down, preferred_element_type=jnp.float32)
+def exchange(blocks):
+    return lax.all_to_all(blocks, "dev", 0, 0, tiled=True)
+
+
+def slot_tables(routes):
+    expert_ids = jnp.arange(2 * GROUPS, dtype=jnp.int32)
+    chosen = jnp.any(routes[:, :, None] == expert_ids, axis=1)
+    earlier = jnp.tri(routes.shape[0], k=-1, dtype=jnp.bfloat16)
+    rank = jnp.dot(earlier, chosen.astype(jnp.bfloat16), preferred_element_type=jnp.float32)
+    return jnp.where(chosen, rank.astype(jnp.int32), -1).T
+
+
+def one_hot(ranks):
+    slot_ids = jnp.arange(CAP, dtype=jnp.int32)[None, :, None]
+    return (ranks[:, None, :] == slot_ids).astype(jnp.bfloat16)
 
 
 def shards(
@@ -89,22 +93,63 @@
     w_up,
     w_down,
 ):
+    row_count = routes.shape[0]
+    core = lax.axis_index("sec") % 2
+    group = lax.axis_index("dev")
     attn = attend(queries, fresh_key_value, key_value_cache, lengths)
+    gain_rows = jnp.pad(three_terms(norm_gain), ((0, attn.shape[0] - 3), (0, 0)))
+    block = jnp.concatenate([attn, gain_rows], axis=1)
+    gathered = exchange(jnp.broadcast_to(block, (GROUPS,) + block.shape))
+    gain = jnp.sum(gathered[:, :3, attn.shape[1] :].astype(jnp.float32), axis=1)
     partial_out = jnp.dot(
-        lax.all_gather(attn, "dev", axis=0, tiled=True),
+        gathered[:, :, : attn.shape[1]].reshape(row_count, attn.shape[1]),
         out_weight,
         preferred_element_type=jnp.float32,
     )
-    hidden = residual.astype(jnp.float32) + lax.psum(partial_out, "sec")
-    square_sum = lax.psum(jnp.sum(hidden * hidden, axis=-1, keepdims=True), "dev")
-    normed = (hidden * lax.rsqrt(square_sum / D + 1e-06) * norm_gain).astype(jnp.bfloat16)
-    full_rows = lax.all_gather(normed, "dev", axis=1, tiled=True)
-    local_count = w_gate.shape[0]
-    local_ids = lax.axis_index("dev") * local_count + jnp.arange(local_count, dtype=jnp.int32)
-    slot_mask, spread = slot_layout(routes, route_weights, local_ids)
-    result = expert_results(full_rows, slot_mask, w_gate, w_up, w_down)
-    expert_term = jnp.einsum("ecr,ecd->rd", spread, result, precision=lax.Precision.HIGHEST)
-    mixture = lax.psum(lax.psum_scatter(expert_term, "dev", scatter_dimension=1, tiled=True), "sec")
+    hidden = residual.astype(jnp.float32) + jnp.sum(lax.all_gather(partial_out, "sec"), axis=0)
+
+    ranks = slot_tables(routes).reshape(GROUPS, 2, row_count)
+    own_ranks = lax.dynamic_index_in_dim(ranks, core, 1, keepdims=False)
+    other_ranks = lax.dynamic_index_in_dim(ranks, 1 - core, 1, keepdims=False)
+    sent = jnp.einsum(
+        "ekr,rf->ekf", one_hot(own_ranks), hidden.astype(jnp.bfloat16), preferred_element_type=jnp.float32
+    ).astype(jnp.bfloat16)
+    own_rows = exchange(sent)
+    other_rows = lax.ppermute(own_rows, "sec", CORE_SWAP)
+
+    local_ids = 2 * group + jnp.arange(2, dtype=jnp.int32)
+    local_ranks = lax.dynamic_index_in_dim(ranks, group, 0, keepdims=False)
+    shares = jnp.sum(
+        jnp.where(routes[None] == local_ids[:, None, None], route_weights[None], 0.0), axis=2
+    )
+    slot_share = jnp.sum(
+        jnp.where(
+            local_ranks[:, None, :] == jnp.arange(CAP, dtype=jnp.int32)[None, :, None],
+            shares[:, None, :],
+            0.0,
+        ),
+        axis=2,
+    )
+
+    rows = jnp.where(core == 0, jnp.stack([own_rows, other_rows]), jnp.stack([other_rows, own_rows]))
+    rows = rows.astype(jnp.float32)
+    square = jnp.sum(rows * rows, axis=(1, 3), keepdims=True)
+    normed = rows * lax.rsqrt(square / D + 1e-06) * gain[None, :, None, :]
+    picked = normed.astype(jnp.bfloat16).transpose(0, 2, 1, 3).reshape(2, CAP, D)
+    gate_part = jnp.einsum("ecd,edf->ecf", picked, w_gate, preferred_element_type=jnp.float32)
+    upward = jnp.einsum("ecd,edf->ecf", picked, w_up, preferred_element_type=jnp.float32)
+    activation = (jax.nn.silu(gate_part) * upward).astype(jnp.bfloat16)
+    result = jnp.einsum("ecf,efd->ecd", activation, w_down, preferred_element_type=jnp.float32)
+    result = result * slot_share[:, :, None]
+    own_result = lax.dynamic_index_in_dim(result, core, 0, keepdims=False)
+    other_result = lax.dynamic_index_in_dim(result, 1 - core, 0, keepdims=False)
+    moved = lax.ppermute(own_result.astype(jnp.bfloat16), "sec", CORE_SWAP)
+    summed = (other_result + moved.astype(jnp.float32)).astype(jnp.bfloat16)
+    returned = exchange(summed.reshape(CAP, GROUPS, D // GROUPS).transpose(1, 0, 2))
+    mixture_part = jnp.einsum(
+        "ekr,ekf->rf", one_hot(other_ranks), returned, preferred_element_type=jnp.float32
+    )
+    mixture = jnp.sum(lax.all_gather(mixture_part, "sec"), axis=0)
     return (hidden + mixture).astype(jnp.bfloat16)
 
 

time: 654 us -> 107 us (0.16)
  waiting for transfers between devices: 520 us -> 44.3 us
  blocking collectives: 81.9 us -> 16.8 us
  starting transfers between devices: 0.17 us -> 18.6 us
  between operations: 13.2 us -> 0.28 us
  matrix products: 28.3 us -> 18.8 us
    all_gather x2 -> x0, waiting for transfers between devices: 273 us -> none  [the longest x1 154 us: shards(): lax.all_gather(attn, 'dev', axis=0, tiled=True)]
    reduce_scatter x1 -> x0, waiting for transfers between devices: 168 us -> none  [shards(): lax.psum_scatter(expert_term, 'dev', scatter_dimension=1, tiled=True)]
    psum x1 -> x0, blocking collectives: 81.9 us -> none  [shards(): lax.psum(jnp.sum(hidden * hidden, axis=-1, keepdims=True), 'dev')]
    psum x2 -> x0, waiting for transfers between devices: 78.8 us -> none  [the longest x1 40.2 us: shards(): hidden = residual.astype(jnp.float32) + lax.psum(partial_out, 'sec')]
    all_to_all x0 -> x3, waiting for transfers between devices: none -> 40.9 us  [exchange(): return lax.all_to_all(blocks, 'dev', 0, 0, tiled=True)]
    all_to_all x0 -> x3, starting transfers between devices: none -> 18.3 us  [exchange(): return lax.all_to_all(blocks, 'dev', 0, 0, tiled=True)]
    all_gather x0 -> x2, blocking collectives: none -> 16.8 us  [the longest x1 8.58 us: shards(): lax.all_gather(partial_out, 'sec')]
    dot_general x5 -> x6, matrix products: 23 us -> 13.5 us  [the longest x1 6.89 us: shards(): jnp.einsum('ecf,efd->ecd', activation, w_down, preferred_element_type=jnp...]
  transfers between devices with their start and end apart: 5 -> 5, of which waited for: 5 -> 5; matrix products, arithmetic and copies ran while one was open for 0% -> 1% of each run, Pallas kernels for 0% -> 0%
where the time goes in v1:
time: 107 us; the launch traced here: 105 us
  waiting for transfers between devices  44.3 us (41%)
  matrix products  18.8 us (18%)
  starting transfers between devices  18.6 us (17%)
  blocking collectives  16.8 us (16%)
  other arithmetic  4.83 us (5%)
  local copies, waits for them, and re-layouts  1.6 us (1%)
    all_to_all x3, waiting for transfers between devices, exchange(): return lax.all_to_all(blocks, 'dev', 0, 0, tiled=True)  40.9 us
    all_to_all x3, starting transfers between devices, exchange(): return lax.all_to_all(blocks, 'dev', 0, 0, tiled=True)  18.3 us
    all_gather x1, blocking collectives, shards(): lax.all_gather(partial_out, 'sec')  8.58 us
    all_gather x1, blocking collectives, shards(): mixture = jnp.sum(lax.all_gather(mixture_part, 'sec'), axis=0)  8.17 us
    dot_general x1, matrix products, shards(): jnp.einsum('ecf,efd->ecd', activation, w_down, preferred_element_type=jnp...  6.89 us
    dot_general x1, matrix products, shards(): jnp.einsum('ecd,edf->ecf', picked, w_gate, preferred_element_type=jnp.flo...  3.9 us
    dot_general x1, matrix products, attend(): jnp.einsum('rkgd,rtkd->rkgt', head_queries, cached_keys, preferred_elemen...  2.35 us
  transfers between devices with their start and end apart: 5, of which 5 were waited for; matrix products, arithmetic and copies ran while one was open for 1% of the time, Pallas kernels for 0%

profile of v1, /device:TPU:0, one launch (start us, length us, event | category | flops | bytes accessed | tf_op | source)
XLA Modules:
  0.0 105.1 jit_solution(4940700587979906806)
XLA Ops:
  0.0 0.7 fusion.70
  0.7 0.7 bitcast_convert_fusion
  1.4 0.7 iota_compare_fusion.12
  2.2 0.9 fusion.61
  3.0 2.4 %select_reduce_fusion = (f32[8,16]{1,0:T(8,128)S(1)}, f32[8,16,1024]{2,1,0:T(8,128)S(1)}) fusion(pred[8,1024]{1,0:T(8,128)(4,1)S(1)} %iota_compare_fusion.12, bf16[2,8,1024,128]{3,2,1,0:T(8,128)(2,1)} %param.14, bf16[8,16,128]{2,0,1:T(8,128)(2,1)} %bitcast.108), kind=kOutput, calls=%fused_computation.46 | convolution fusion | flops 33947520 | bytes 2662912 | tf_op jit(solution)/shard_map/rkgd,rtkd->rkgt/dot_general | solution.py:29
  5.7 2.1 %fusion.27 = bf16[1,8,16,128]{3,2,1,0:T(8,128)(2,1)S(1)} fusion(bf16[2,8,1024,128]{3,2,1,0:T(8,128)(2,1)} %param.14, f32[8,16,1024]{2,1,0:T(8,128)S(1)} %get-tuple-element.15, f32[8,16]{1,0:T(8,128)S(1)} %multiply_maximum_fusion, pred[8,1024]{1,0:T(8,128)(4,1)S(1)} %iota_compare_fusion.12, f32[8,16]{1,0:T(8,128)S(1)} %get-tuple-element.5, ...), kind=kOutput, calls=%fused_computation.26 | convolution fusion | flops 34013184 | bytes 2668032 | tf_op jit(solution)/shard_map/rkgt,rtkd->rkgd/dot_general | solution.py:43
  7.8 1.1 %broadcast_in_dim.74 = bf16[32,8,2176]{2,1,0:T(8,128)(2,1)} broadcast(bf16[8,2176]{1,0:T(8,128)(2,1)S(1)} %pad_maximum_fusion), dimensions={1,2} | broadcast | bytes 1148928 | tf_op jit(solution)/shard_map/broadcast_in_dim | solution.py:102
  8.9 9.3 %all-to-all-start = ((bf16[32,8,2176]{2,1,0:T(8,128)(2,1)}), bf16[32,8,2176]{2,1,0:T(8,128)(2,1)S(1)}, u32[]{:S(2)}, u32[]{:S(2)}) async-start(bf16[32,8,2176]{2,1,0:T(8,128)(2,1)} %broadcast_in_dim.74), calls=%async_computation | async-start | bytes 2228224 | tf_op jit(solution)/shard_map/all_to_all | solution.py:66
  18.7 16.9 %all-to-all-done = bf16[32,8,2176]{2,1,0:T(8,128)(2,1)S(1)} async-done(((bf16[32,8,2176]{2,1,0:T(8,128)(2,1)}), bf16[32,8,2176]{2,1,0:T(8,128)(2,1)S(1)}, u32[]{:S(2)}, u32[]{:S(2)}) %all-to-all-start) | async-done | bytes 1114144 | tf_op jit(solution)/shard_map/all_to_all | solution.py:66
  36.0 8.6 %all-gather = f32[1024,128]{1,0:T(8,128)S(1)} all-gather(f32[256,128]{1,0:T(8,128)S(1)} %fusion.35), channel_id=2, replica_groups=mesh['sec'=4,'dev'=32] {'sec'}, dimensions={0}, use_global_device_ids=true | all-gather | bytes 655360 | tf_op jit(solution)/shard_map/all_gather | solution.py:109
  44.6 1.3 %fusion.11 = bf16[32,64,128]{2,1,0:T(8,128)(2,1)} fusion(s32[32,256]{1,0:T(8,128)S(1)} %bitcast.105, f32[256,128]{1,0:T(8,128)S(1)} %reduce_sum.64, bf16[256,128]{1,0:T(8,128)(2,1)S(1)} %copy-done.2), kind=kOutput, calls=%fused_computation.16 | convolution fusion | flops 135102464 | bytes 753664 | tf_op jit(solution)/shard_map/ekr,rf->ekf/dot_general | solution.py:114
  45.9 4.8 %all-to-all-start.1 = ((bf16[32,64,128]{2,1,0:T(8,128)(2,1)}), bf16[32,64,128]{2,1,0:T(8,128)(2,1)S(1)}, u32[]{:S(2)}, u32[]{:S(2)}) async-start(bf16[32,64,128]{2,1,0:T(8,128)(2,1)} %fusion.11), calls=%async_computation.1 | async-start | bytes 1048576 | tf_op jit(solution)/shard_map/all_to_all | solution.py:66
  50.6 12.1 %all-to-all-done.1 = bf16[32,64,128]{2,1,0:T(8,128)(2,1)S(1)} async-done(((bf16[32,64,128]{2,1,0:T(8,128)(2,1)}), bf16[32,64,128]{2,1,0:T(8,128)(2,1)S(1)}, u32[]{:S(2)}, u32[]{:S(2)}) %all-to-all-start.1) | async-done | bytes 524320 | tf_op jit(solution)/shard_map/all_to_all | solution.py:66
  63.0 1.7 %collective-permute-done = bf16[32,64,128]{2,1,0:T(8,128)(2,1)S(1)} collective-permute-done((bf16[32,64,128]{2,1,0:T(8,128)(2,1)S(1)}, bf16[32,64,128]{2,1,0:T(8,128)(2,1)S(1)}, u32[]{:S(2)}, u32[]{:S(2)}) %collective-permute-start) | collective-permute-done | bytes 524320 | tf_op jit(solution)/shard_map/ppermute | solution.py:118
  64.7 0.5 fusion
  65.4 3.9 %fusion.33 = f32[2,64,384]{2,1,0:T(8,128)S(1)} fusion(bf16[2,4096,384]{2,1,0:T(8,128)(2,1)} %param.21, f32[32,128]{1,0:T(8,128)S(1)} %convert_reduce_fusion, f32[2,64]{1,0:T(2,128)S(1)} %add_rsqrt_fusion, bf16[1,32,64,128]{3,2,1,0:T(8,128)(2,1)S(1)} %bitcast.97, bf16[1,32,64,128]{3,2,1,0:T(8,128)(2,1)S(1)} %bitcast.100, pred[]{:T(512)S(6)} %eq.83), kind=kOutput, calls=%fused_computation.29 | convolution fusion | flops 406323200 | bytes 7553537 | tf_op jit(solution)/shard_map/ecd,edf->ecf/dot_general | solution.py:139
  69.4 6.9 %convolution_multiply_fusion = f32[2,64,4096]{2,1,0:T(8,128)S(1)} fusion(bf16[2,384,4096]{2,1,0:T(8,128)(2,1)} %param.23, bf16[2,4096,384]{2,1,0:T(8,128)(2,1)} %param.22, f32[2,64]{1,0:T(2,128)S(1)} %select_reduce_fusion.1, f32[2,64,384]{2,1,0:T(8,128)S(1)} %fusion.33, f32[32,128]{1,0:T(8,128)S(1)} %convert_reduce_fusion, f32[2,64]{1,0:T(2,128)S(1)} %add_rsqrt_fusion, ...), kind=kOutput, calls=%fused_computation | convolution fusion | flops 809795584 | bytes 15942657 | tf_op jit(solution)/shard_map/ecf,efd->ecd/dot_general | solution.py:142
  76.5 1.8 %collective-permute-done.1 = bf16[64,4096]{1,0:T(8,128)(2,1)S(1)} collective-permute-done((bf16[64,4096]{1,0:T(8,128)(2,1)S(1)}, bf16[64,4096]{1,0:T(8,128)(2,1)S(1)}, u32[]{:S(2)}, u32[]{:S(2)}) %collective-permute-start.1) | collective-permute-done | bytes 524320 | tf_op jit(solution)/shard_map/ppermute | solution.py:146
  78.3 0.9 bitcast_bitcast_fusion
  79.3 4.3 %all-to-all-start.2 = ((bf16[32,64,128]{2,1,0:T(8,128)(2,1)}), bf16[32,64,128]{2,1,0:T(8,128)(2,1)S(1)}, u32[]{:S(2)}, u32[]{:S(2)}) async-start(bf16[32,64,128]{2,1,0:T(8,128)(2,1)} %bitcast_bitcast_fusion), calls=%async_computation.2 | async-start | bytes 1048576 | tf_op jit(solution)/shard_map/all_to_all | solution.py:66
  83.6 11.9 %all-to-all-done.2 = bf16[32,64,128]{2,1,0:T(8,128)(2,1)S(1)} async-done(((bf16[32,64,128]{2,1,0:T(8,128)(2,1)}), bf16[32,64,128]{2,1,0:T(8,128)(2,1)S(1)}, u32[]{:S(2)}, u32[]{:S(2)}) %all-to-all-start.2) | async-done | bytes 524320 | tf_op jit(solution)/shard_map/all_to_all | solution.py:66
  95.5 0.7 fusion.16
  96.2 8.2 %all-gather.1 = f32[1024,128]{1,0:T(8,128)S(1)} all-gather(f32[256,128]{1,0:T(8,128)S(1)} %fusion.16), channel_id=3, replica_groups=mesh['sec'=4,'dev'=32] {'sec'}, dimensions={0}, use_global_device_ids=true | all-gather | bytes 655360 | tf_op jit(solution)/shard_map/all_gather | solution.py:152
  104.4 0.7 add_convert_fusion
  (38 shorter events, 2.0 us)
Async XLA Ops:
  0.0 35.5 %copy-start = (bf16[2048,128]{1,0:T(8,128)(2,1)S(1)}, bf16[2048,128]{1,0:T(8,128)(2,1)}, u32[]{:S(2)}) copy-start(bf16[2048,128]{1,0:T(8,128)(2,1)} %param.17) | copy-start | bytes 1572868
  7.7 10.4 %copy-start.4 = (s32[256,8]{0,1:T(8,128)S(1)}, s32[256,8]{0,1:T(8,128)}, u32[]{:S(2)}) copy-start(s32[256,8]{0,1:T(8,128)} %param.19) | copy-start | bytes 24580
  8.9 26.7 %all-to-all-start = ((bf16[32,8,2176]{2,1,0:T(8,128)(2,1)}), bf16[32,8,2176]{2,1,0:T(8,128)(2,1)S(1)}, u32[]{:S(2)}, u32[]{:S(2)}) async-start(bf16[32,8,2176]{2,1,0:T(8,128)(2,1)} %broadcast_in_dim.74), calls=%async_computation | async-start | bytes 2228224 | tf_op jit(solution)/shard_map/all_to_all | solution.py:66
  18.1 26.5 %copy-start.2 = (bf16[256,128]{1,0:T(8,128)(2,1)S(1)}, bf16[256,128]{1,0:T(8,128)(2,1)}, u32[]{:S(2)}) copy-start(bf16[256,128]{1,0:T(8,128)(2,1)} %param.16) | copy-start | bytes 196612
  36.0 26.8 %copy-start.5 = (f32[256,8]{0,1:T(8,128)S(1)}, f32[256,8]{0,1:T(8,128)}, u32[]{:S(2)}) copy-start(f32[256,8]{0,1:T(8,128)} %param.20) | copy-start | bytes 24580
  45.9 16.9 %all-to-all-start.1 = ((bf16[32,64,128]{2,1,0:T(8,128)(2,1)}), bf16[32,64,128]{2,1,0:T(8,128)(2,1)S(1)}, u32[]{:S(2)}, u32[]{:S(2)}) async-start(bf16[32,64,128]{2,1,0:T(8,128)(2,1)} %fusion.11), calls=%async_computation.1 | async-start | bytes 1048576 | tf_op jit(solution)/shard_map/all_to_all | solution.py:66
  62.7 1.9 %collective-permute-start = (bf16[32,64,128]{2,1,0:T(8,128)(2,1)S(1)}, bf16[32,64,128]{2,1,0:T(8,128)(2,1)S(1)}, u32[]{:S(2)}, u32[]{:S(2)}) collective-permute-start(bf16[32,64,128]{2,1,0:T(8,128)(2,1)S(1)} %all-to-all-done.1), channel_id=1, source_target_pairs={{0,32},{32,0},{64,96},{96,64},{1,33},{33,1},{65,97},{97,65},{2,34}... | collective-permute-start | bytes 1572872 | tf_op jit(solution)/shard_map/ppermute | solution.py:118
  64.7 0.8 copy-start.1
  76.3 2.0 %collective-permute-start.1 = (bf16[64,4096]{1,0:T(8,128)(2,1)S(1)}, bf16[64,4096]{1,0:T(8,128)(2,1)S(1)}, u32[]{:S(2)}, u32[]{:S(2)}) collective-permute-start(bf16[64,4096]{1,0:T(8,128)(2,1)S(1)} %fusion.42), channel_id=1, source_target_pairs={{0,32},{32,0},{64,96},{96,64},{1,33},{33,1},{65,97},{97,65},{2,34}... | collective-permute-start | bytes 1572872 | tf_op jit(solution)/shard_map/ppermute | solution.py:146
  79.3 25.2 %copy-start.3 = (bf16[256,128]{1,0:T(8,128)(2,1)S(1)}, bf16[256,128]{1,0:T(8,128)(2,1)}, u32[]{:S(2)}) copy-start(bf16[256,128]{1,0:T(8,128)(2,1)} %param.16) | copy-start | bytes 196612
  79.3 16.2 %all-to-all-start.2 = ((bf16[32,64,128]{2,1,0:T(8,128)(2,1)}), bf16[32,64,128]{2,1,0:T(8,128)(2,1)S(1)}, u32[]{:S(2)}, u32[]{:S(2)}) async-start(bf16[32,64,128]{2,1,0:T(8,128)(2,1)} %bitcast_bitcast_fusion), calls=%async_computation.2 | async-start | bytes 1048576 | tf_op jit(solution)/shard_map/all_to_all | solution.py:66

commit v2 on v1

v2 whole, which is shorter than its diff:
```python
import math

import jax
import jax.numpy as jnp
from jax import lax
from jax.experimental import pallas as pl
from jax.experimental.pallas import tpu as pltpu
from jax.sharding import PartitionSpec as P

D = 4096
QUERY_HEADS = 64
KEY_VALUE_HEADS = 4
HEAD_SIZE = 128
CAP = 64
GROUPS = 32
CHUNKS = 4
CORE_SWAP = [(0, 1), (1, 0), (2, 3), (3, 2)]


def attend_kernel(
    lengths_hbm,
    queries_hbm,
    fresh_hbm,
    gain_hbm,
    cache_ref,
    block_ref,
    lengths_ref,
    queries_ref,
    fresh_ref,
    gain_ref,
    keys,
    values,
    head_queries,
    head_scores,
    head_outputs,
    staged,
    small_sems,
    key_sems,
    value_sems,
    block_sems,
):
    rows = queries_ref.shape[0]
    heads = queries_ref.shape[1] // HEAD_SIZE
    slots = keys.shape[1]
    scale = 1.0 / math.sqrt(HEAD_SIZE)
    key_copies = [
        pltpu.make_async_copy(cache_ref.at[0, r], keys.at[r], key_sems.at[r]) for r in range(rows)
    ]
    value_copies = [
        pltpu.make_async_copy(cache_ref.at[1, r], values.at[r], value_sems.at[r])
        for r in range(rows)
    ]
    small_copies = [
        pltpu.make_async_copy(source, target, small_sems.at[i])
        for i, (source, target) in enumerate(
            (
                (queries_hbm, queries_ref),
                (gain_hbm, gain_ref),
                (fresh_hbm, fresh_ref),
                (lengths_hbm, lengths_ref),
            )
        )
    ]
    for copy in small_copies + key_copies + value_copies:
        copy.start()
    for copy in small_copies:
        copy.wait()
    gain = gain_ref[...]
    high = gain.astype(jnp.bfloat16).astype(jnp.float32)
    middle = (gain - high).astype(jnp.bfloat16).astype(jnp.float32)
    low = gain - high - middle
    place = lax.broadcasted_iota(jnp.int32, (rows, HEAD_SIZE), 0)
    terms = jnp.where(
        place == 0, high, jnp.where(place == 1, middle, jnp.where(place == 2, low, 0.0))
    )
    staged[:, heads * HEAD_SIZE :] = terms.astype(jnp.bfloat16)
    for h in range(heads):
        head_queries[pl.ds(h, rows, stride=heads), :] = queries_ref[
            :, h * HEAD_SIZE : (h + 1) * HEAD_SIZE
        ].astype(jnp.float32)
    for r in range(rows):
        key_copies[r].wait()
        head_scores[r * heads : (r + 1) * heads, :] = lax.dot_general(
            head_queries[r * heads : (r + 1) * heads, :].astype(jnp.bfloat16),
            keys[r],
            (((1,), (1,)), ((), ())),
            preferred_element_type=jnp.float32,
        )
    slot = lax.broadcasted_iota(jnp.int32, (heads, slots), 1)
    weights, own_weights, normalizers = [], [], []
    for r in range(rows):
        own_key = fresh_ref[0, r : r + 1, :].astype(jnp.float32)
        own_score = (
            jnp.sum(
                head_queries[r * heads : (r + 1) * heads, :] * own_key, axis=1, keepdims=True
            )
            * scale
        )
        scores = jnp.where(
            slot < lengths_ref[r], head_scores[r * heads : (r + 1) * heads, :] * scale, -jnp.inf
        )
        row_max = jnp.maximum(jnp.max(scores, axis=1, keepdims=True), own_score)
        weight = jnp.exp(scores - row_max)
        own_weight = jnp.exp(own_score - row_max)
        normalizers.append(jnp.sum(weight, axis=1, keepdims=True) + own_weight)
        weights.append(weight.astype(jnp.bfloat16))
        own_weights.append(own_weight)
    for r in range(rows):
        value_copies[r].wait()
        own_value = fresh_ref[1, r : r + 1, :].astype(jnp.float32)
        weighted = jnp.dot(weights[r], values[r], preferred_element_type=jnp.float32)
        head_outputs[r * heads : (r + 1) * heads, :] = (
            weighted + own_weights[r] * own_value
        ) / normalizers[r]
    for h in range(heads):
        staged[:, h * HEAD_SIZE : (h + 1) * HEAD_SIZE] = head_outputs[
            pl.ds(h, rows, stride=heads), :
        ].astype(jnp.bfloat16)
    block_copies = [
        pltpu.make_async_copy(staged, block_ref.at[i], block_sems.at[i])
        for i in range(block_ref.shape[0])
    ]
    for copy in block_copies:
        copy.start()
    for copy in block_copies:
        copy.wait()


def attend(queries, fresh_key_value, key_value_cache, lengths, norm_gain):
    rows, width = queries.shape
    slots = key_value_cache.shape[2]
    heads = width // HEAD_SIZE
    operands = (lengths, queries, fresh_key_value, norm_gain.reshape(1, HEAD_SIZE), key_value_cache)
    return pl.pallas_call(
        attend_kernel,
        out_shape=jax.ShapeDtypeStruct((GROUPS, rows, width + HEAD_SIZE), jnp.bfloat16),
        in_specs=[pl.BlockSpec(memory_space=pl.ANY)] * len(operands),
        out_specs=pl.BlockSpec(memory_space=pl.ANY),
        scratch_shapes=[
            pltpu.SMEM((rows,), jnp.int32),
            pltpu.VMEM(queries.shape, jnp.bfloat16),
            pltpu.VMEM(fresh_key_value.shape, jnp.bfloat16),
            pltpu.VMEM((1, HEAD_SIZE), jnp.float32),
            pltpu.VMEM((rows, slots, HEAD_SIZE), jnp.bfloat16),
            pltpu.VMEM((rows, slots, HEAD_SIZE), jnp.bfloat16),
            pltpu.VMEM((rows * heads, HEAD_SIZE), jnp.float32),
            pltpu.VMEM((rows * heads, slots), jnp.float32),
            pltpu.VMEM((rows * heads, HEAD_SIZE), jnp.float32),
            pltpu.VMEM((rows, width + HEAD_SIZE), jnp.bfloat16),
            pltpu.SemaphoreType.DMA((4,)),
            pltpu.SemaphoreType.DMA((rows,)),
            pltpu.SemaphoreType.DMA((rows,)),
            pltpu.SemaphoreType.DMA((GROUPS,)),
        ],
        compiler_params=pltpu.CompilerParams(vmem_limit_bytes=12 << 20),
        cost_estimate=pl.CostEstimate(
            flops=4 * rows * heads * slots * HEAD_SIZE,
            bytes_accessed=5 << 20,
            transcendentals=rows * heads * slots,
        ),
        name="attend",
    )(*(pltpu.with_memory_space_constraint(operand, pltpu.HBM) for operand in operands))


def fill_picked(rows_ref, gain_ref, picked):
    groups, cap, width = rows_ref.shape
    square = jnp.zeros((cap, width), jnp.float32)
    for g in range(groups):
        part = rows_ref[g].astype(jnp.float32)
        square = square + part * part
    factor = lax.rsqrt(jnp.sum(square, axis=1, keepdims=True) / D + 1e-06)
    for g in range(groups):
        part = rows_ref[g].astype(jnp.float32)
        picked[:, g * width : (g + 1) * width] = (
            part * factor * gain_ref[g : g + 1, :]
        ).astype(jnp.bfloat16)


def row_copies(source, expert, target, sems):
    count, size = target.shape[0], target.shape[1]
    return [
        pltpu.make_async_copy(
            source.at[expert, pl.ds(k * size, size)], target.at[k], sems.at[k]
        )
        for k in range(count)
    ]


def column_copies(source, expert, target, sems):
    count, size = target.shape[0], target.shape[2]
    return [
        pltpu.make_async_copy(
            source.at[expert, :, pl.ds(k * size, size)], target.at[k], sems.at[k]
        )
        for k in range(count)
    ]


def activate(picked, gate, gate_copies, up, up_copies):
    size = gate.shape[1]
    gate_part = jnp.zeros((CAP, gate.shape[2]), jnp.float32)
    upward = gate_part
    for k in range(gate.shape[0]):
        part = picked[:, k * size : (k + 1) * size]
        gate_copies[k].wait()
        gate_part = gate_part + jnp.dot(part, gate[k], preferred_element_type=jnp.float32)
        up_copies[k].wait()
        upward = upward + jnp.dot(part, up[k], preferred_element_type=jnp.float32)
    return (gate_part / (1.0 + jnp.exp(-gate_part)) * upward).astype(jnp.bfloat16)


def own_expert_kernel(
    rows_ref, gain_ref, share_ref, gate_hbm, up_hbm, down_hbm, out_ref, picked, gate, up, down, sems
):
    expert = lax.rem(lax.axis_index("sec"), 2)
    gate_copies = row_copies(gate_hbm, expert, gate, sems.at[0])
    up_copies = row_copies(up_hbm, expert, up, sems.at[1])
    down_copies = column_copies(down_hbm, expert, down, sems.at[2])
    for gate_copy, up_copy in zip(gate_copies, up_copies):
        gate_copy.start()
        up_copy.start()
    for copy in down_copies:
        copy.start()
    fill_picked(rows_ref, gain_ref, picked)
    activation = activate(picked, gate, gate_copies, up, up_copies)
    share = share_ref[expert]
    step = down.shape[2]
    for k, copy in enumerate(down_copies):
        copy.wait()
        part = jnp.dot(activation, down[k], preferred_element_type=jnp.float32)
        out_ref[:, k * step : (k + 1) * step] = (part * share).astype(jnp.bfloat16)


def other_gate_kernel(rows_ref, gain_ref, gate_hbm, up_hbm, out_ref, picked, gate, up, sems):
    expert = 1 - lax.rem(lax.axis_index("sec"), 2)
    gate_copies = row_copies(gate_hbm, expert, gate, sems.at[0])
    up_copies = row_copies(up_hbm, expert, up, sems.at[1])
    for gate_copy, up_copy in zip(gate_copies, up_copies):
        gate_copy.start()
        up_copy.start()
    fill_picked(rows_ref, gain_ref, picked)
    out_ref[...] = activate(picked, gate, gate_copies, up, up_copies)


def other_down_kernel(activation_ref, moved_ref, share_ref, down_hbm, out_ref, down, sems):
    expert = 1 - lax.rem(lax.axis_index("sec"), 2)
    down_copies = column_copies(down_hbm, expert, down, sems.at[0])
    for copy in down_copies:
        copy.start()
    share = share_ref[expert]
    activation = activation_ref[...]
    width = out_ref.shape[2]
    step = down.shape[2]
    for k, copy in enumerate(down_copies):
        copy.wait()
        part = jnp.dot(activation, down[k], preferred_element_type=jnp.float32)
        part = part * share + moved_ref[:, k * step : (k + 1) * step].astype(jnp.float32)
        for g in range(step // width):
            out_ref[k * step // width + g] = part[:, g * width : (g + 1) * width].astype(
                jnp.bfloat16
            )


def expert_call(kernel, name, out_shape, scratch, small, weights):
    vmem = pl.BlockSpec(memory_space=pltpu.VMEM)
    any_space = pl.BlockSpec(memory_space=pl.ANY)
    size = sum(weight.size // 2 for weight in weights)
    sems = pltpu.SemaphoreType.DMA((len(weights), CHUNKS))
    return pl.pallas_call(
        kernel,
        out_shape=jax.ShapeDtypeStruct(out_shape, jnp.bfloat16),
        in_specs=[vmem] * len(small) + [any_space] * len(weights),
        out_specs=vmem,
        scratch_shapes=[pltpu.VMEM(shape, jnp.bfloat16) for shape in scratch] + [sems],
        compiler_params=pltpu.CompilerParams(vmem_limit_bytes=20 << 20),
        cost_estimate=pl.CostEstimate(
            flops=2 * CAP * size, bytes_accessed=2 * size, transcendentals=0
        ),
        name=name,
    )(
        *(pltpu.with_memory_space_constraint(array, pltpu.VMEM) for array in small),
        *(pltpu.with_memory_space_constraint(array, pltpu.HBM) for array in weights),
    )


def exchange(blocks):
    return lax.all_to_all(blocks, "dev", 0, 0, tiled=True)


def slot_tables(routes):
    expert_ids = jnp.arange(2 * GROUPS, dtype=jnp.int32)
    chosen = jnp.any(routes[:, :, None] == expert_ids, axis=1)
    earlier = jnp.tri(routes.shape[0], k=-1, dtype=jnp.bfloat16)
    rank = jnp.dot(earlier, chosen.astype(jnp.bfloat16), preferred_element_type=jnp.float32)
    return jnp.where(chosen, rank.astype(jnp.int32), -1).T


def one_hot(ranks):
    slot_ids = jnp.arange(CAP, dtype=jnp.int32)[None, :, None]
    return (ranks[:, None, :] == slot_ids).astype(jnp.bfloat16)


def shards(
    queries,
    fresh_key_value,
    key_value_cache,
    lengths,
    residual,
    out_weight,
    norm_gain,
    routes,
    route_weights,
    w_gate,
    w_up,
    w_down,
):
    row_count = routes.shape[0]
    width = queries.shape[1]
    core = lax.axis_index("sec") % 2
    group = lax.axis_index("dev")
    blocks = attend(queries, fresh_key_value, key_value_cache, lengths, norm_gain)
    gathered = exchange(blocks)
    gain = jnp.sum(gathered[:, :3, width:].astype(jnp.float32), axis=1)
    partial_out = jnp.dot(
        gathered[:, :, :width].reshape(row_count, width),
        out_weight,
        preferred_element_type=jnp.float32,
    )
    hidden = residual.astype(jnp.float32) + jnp.sum(lax.all_gather(partial_out, "sec"), axis=0)

    ranks = slot_tables(routes).reshape(GROUPS, 2, row_count)
    own_ranks = lax.dynamic_index_in_dim(ranks, core, 1, keepdims=False)
    other_ranks = lax.dynamic_index_in_dim(ranks, 1 - core, 1, keepdims=False)
    sent = jnp.einsum(
        "ekr,rf->ekf", one_hot(own_ranks), hidden.astype(jnp.bfloat16), preferred_element_type=jnp.float32
    ).astype(jnp.bfloat16)
    own_rows = exchange(sent)
    other_rows = lax.ppermute(own_rows, "sec", CORE_SWAP)

    local_ids = 2 * group + jnp.arange(2, dtype=jnp.int32)
    local_ranks = lax.dynamic_index_in_dim(ranks, group, 0, keepdims=False)
    shares = jnp.sum(
        jnp.where(routes[None] == local_ids[:, None, None], route_weights[None], 0.0), axis=2
    )
    slot_share = jnp.sum(
        jnp.where(
            local_ranks[:, None, :] == jnp.arange(CAP, dtype=jnp.int32)[None, :, None],
            shares[:, None, :],
            0.0,
        ),
        axis=2,
    )

    share = slot_share[:, :, None]
    units = w_gate.shape[2]
    picked_shape = (CAP, D)
    gate_shape = (CHUNKS, D // CHUNKS, units)
    down_shape = (CHUNKS, units, D // CHUNKS)
    own_result = expert_call(
        own_expert_kernel,
        "own_expert",
        (CAP, D),
        [picked_shape, gate_shape, gate_shape, down_shape],
        [own_rows, gain, share],
        [w_gate, w_up, w_down],
    )
    moved = lax.ppermute(own_result, "sec", CORE_SWAP)
    activation = expert_call(
        other_gate_kernel,
        "other_gate",
        (CAP, units),
        [picked_shape, gate_shape, gate_shape],
        [other_rows, gain],
        [w_gate, w_up],
    )
    summed = expert_call(
        other_down_kernel,
        "other_down",
        (GROUPS, CAP, D // GROUPS),
        [down_shape],
        [activation, moved, share],
        [w_down],
    )
    returned = exchange(summed)
    mixture_part = jnp.einsum(
        "ekr,ekf->rf", one_hot(other_ranks), returned, preferred_element_type=jnp.float32
    )
    mixture = jnp.sum(lax.all_gather(mixture_part, "sec"), axis=0)
    return (hidden + mixture).astype(jnp.bfloat16)


def solution(mesh):
    return jax.shard_map(
        shards,
        mesh=mesh,
        in_specs=(
            P("dev", "sec"),
            P(None, "dev", "sec"),
            P(None, "dev", None, "sec"),
            P("dev"),
            P(None, "dev"),
            P("sec", "dev"),
            P("dev"),
            P(),
            P(),
            P("dev", None, "sec"),
            P("dev", None, "sec"),
            P("dev", "sec", None),
        ),
        out_specs=P(None, "dev"),
        check_vma=False,
    )
```

time: 107 us -> 99 us (0.925)
  Pallas kernels: 0 us -> 17.1 us
  matrix products: 18.8 us -> 2.67 us
  waiting for transfers between devices: 44.3 us -> 40.4 us
  other arithmetic: 4.83 us -> 1.01 us
  local copies, waits for them, and re-layouts: 1.6 us -> 0.25 us
    pallas_call x0 -> x4, Pallas kernels: none -> 17.1 us  [the longest x3 10.9 us: expert_call(): pl.pallas_call(kernel, out_shape=jax.ShapeDtypeStruct(out_shape, jnp.bflo...]
    dot_general x6 -> x1, matrix products: 16.5 us -> 0.42 us  [shards(): jnp.dot(gathered[:, :, :width].reshape(row_count, width), out_weight, pre...]
    ppermute x1, waiting for transfers between devices: 1.77 us -> 0.01 us  [shards(): moved = lax.ppermute(own_result, 'sec', CORE_SWAP)]
    ppermute x1, waiting for transfers between devices: 1.67 us -> 0.01 us  [shards(): other_rows = lax.ppermute(own_rows, 'sec', CORE_SWAP)]
  transfers between devices with their start and end apart: 5 -> 5, of which waited for: 5 -> 3; matrix products, arithmetic and copies ran while one was open for 1% -> 1% of each run, Pallas kernels for 0% -> 8%
where the time goes in v2:
time: 99 us; the launch traced here: 97.2 us
  waiting for transfers between devices  40.4 us (41%)
  starting transfers between devices  18.8 us (19%)
  Pallas kernels  17.1 us (17%)
  blocking collectives  16.8 us (17%)
  matrix products  2.67 us (3%)
  other arithmetic  1.01 us (1%)
    all_to_all x3, waiting for transfers between devices, exchange(): return lax.all_to_all(blocks, 'dev', 0, 0, tiled=True)  40.4 us
    all_to_all x3, starting transfers between devices, exchange(): return lax.all_to_all(blocks, 'dev', 0, 0, tiled=True)  18.2 us
    pallas_call x3, Pallas kernels, expert_call(): pl.pallas_call(kernel, out_shape=jax.ShapeDtypeStruct(out_shape, jnp.bflo...  10.9 us
    all_gather x1, blocking collectives, shards(): lax.all_gather(partial_out, 'sec')  8.58 us
    all_gather x1, blocking collectives, shards(): mixture = jnp.sum(lax.all_gather(mixture_part, 'sec'), axis=0)  8.17 us
    pallas_call x1, Pallas kernels, attend(): pl.pallas_call(attend_kernel, out_shape=jax.ShapeDtypeStruct((GROUPS, row...  6.19 us
  transfers between devices with their start and end apart: 5, of which 3 were waited for; matrix products, arithmetic and copies ran while one was open for 1% of the time, Pallas kernels for 8%

profile of v2, /device:TPU:0, one launch (start us, length us, event | category | flops | bytes accessed | tf_op | source)
XLA Modules:
  0.0 97.2 jit_solution(10974724710552263388)
XLA Ops:
  0.0 6.2 %attend.1 = bf16[32,8,2176]{2,1,0:T(8,128)(2,1)} custom-call(s32[8]{0:T(128)} %lengths_hbm.1, bf16[8,2048]{1,0:T(8,128)(2,1)} %queries_hbm.1, bf16[2,8,128]{2,1,0:T(8,128)(2,1)} %fresh_hbm.1, f32[1,128]{1,0:T(1,128)} %bitcast.30, bf16[2,8,1024,128]{3,2,1,0:T(8,128)(2,1)} %cache_ref.1), custom_call_target="tpu_custom_call" | custom-call | flops 67108864 | bytes 5242880 | tf_op jit(solution)/shard_map/attend/pallas_call | solution.py:134
  6.2 9.3 %all-to-all-start = ((bf16[32,8,2176]{2,1,0:T(8,128)(2,1)}), bf16[32,8,2176]{2,1,0:T(8,128)(2,1)S(1)}, u32[]{:S(2)}, u32[]{:S(2)}) async-start(bf16[32,8,2176]{2,1,0:T(8,128)(2,1)} %attend.1), calls=%async_computation | async-start | bytes 2228224 | tf_op jit(solution)/shard_map/all_to_all | solution.py:287
  15.5 0.0 copy-start.1
  15.5 0.1 fusion.8
  15.6 0.3 fusion.4
  15.9 0.1 constant_dynamic-slice_fusion.1
  16.0 16.9 %all-to-all-done = bf16[32,8,2176]{2,1,0:T(8,128)(2,1)S(1)} async-done(((bf16[32,8,2176]{2,1,0:T(8,128)(2,1)}), bf16[32,8,2176]{2,1,0:T(8,128)(2,1)S(1)}, u32[]{:S(2)}, u32[]{:S(2)}) %all-to-all-start) | async-done | bytes 1114144 | tf_op jit(solution)/shard_map/all_to_all | solution.py:287
  32.9 0.4 fusion.5
  33.4 8.6 %all-gather = f32[1024,128]{1,0:T(8,128)S(1)} all-gather(f32[256,128]{1,0:T(8,128)S(1)} %fusion.5), channel_id=2, replica_groups=mesh['sec'=4,'dev'=32] {'sec'}, dimensions={0}, use_global_device_ids=true | all-gather | bytes 655360 | tf_op jit(solution)/shard_map/all_gather | solution.py:329
  42.0 1.3 %fusion.2 = bf16[32,64,128]{2,1,0:T(8,128)(2,1)} fusion(s32[32,256]{1,0:T(8,128)S(1)} %bitcast.27, f32[256,128]{1,0:T(8,128)S(1)} %reduce_sum.45, bf16[256,128]{1,0:T(8,128)(2,1)S(1)} %copy-done.1), kind=kOutput, calls=%fused_computation.4 | convolution fusion | flops 135102464 | bytes 753664 | tf_op jit(solution)/shard_map/ekr,rf->ekf/dot_general | solution.py:334
  43.2 4.8 %all-to-all-start.1 = ((bf16[32,64,128]{2,1,0:T(8,128)(2,1)}), bf16[32,64,128]{2,1,0:T(8,128)(2,1)S(1)}, u32[]{:S(2)}, u32[]{:S(2)}) async-start(bf16[32,64,128]{2,1,0:T(8,128)(2,1)} %fusion.2), calls=%async_computation.1 | async-start | bytes 1048576 | tf_op jit(solution)/shard_map/all_to_all | solution.py:287
  48.0 0.1 select_reduce_fusion.1
  48.1 0.1 select_reduce_fusion
  48.2 0.1 copy.18.share_ref
  48.4 11.7 %all-to-all-done.1.rows_ref = bf16[32,64,128]{2,1,0:T(8,128)(2,1)S(1)} async-done(((bf16[32,64,128]{2,1,0:T(8,128)(2,1)}), bf16[32,64,128]{2,1,0:T(8,128)(2,1)S(1)}, u32[]{:S(2)}, u32[]{:S(2)}) %all-to-all-start.1) | async-done | bytes 524320 | tf_op jit(solution)/shard_map/all_to_all | solution.py:287
  60.1 4.5 %own_expert.1 = bf16[64,4096]{1,0:T(8,128)(2,1)S(1)} custom-call(bf16[32,64,128]{2,1,0:T(8,128)(2,1)S(1)} %all-to-all-done.1.rows_ref, f32[32,128]{1,0:T(8,128)S(1)} %convert_reduce_fusion.gain_ref, f32[2,64,1]{2,1,0:T(8,128)S(1)} %copy.18.share_ref, bf16[2,4096,384]{2,1,0:T(8,128)(2,1)} %gate_hbm.3, bf16[2,4096,384]{2,1,0:T(8,128)(2,1)} %up_hbm.3, ...), custom_call_target="tpu_custom_call" | custom-call | flops 603979776 | bytes 9437184 | tf_op jit(solution)/shard_map/own_expert/pallas_call | solution.py:269
  64.7 0.6 collective-permute-start.1
  65.2 3.4 %other_gate.1.activation_ref = bf16[64,384]{1,0:T(8,128)(2,1)S(1)} custom-call(bf16[32,64,128]{2,1,0:T(8,128)(2,1)S(1)} %collective-permute-done.rows_ref, f32[32,128]{1,0:T(8,128)S(1)} %convert_reduce_fusion.gain_ref, bf16[2,4096,384]{2,1,0:T(8,128)(2,1)} %gate_hbm.3, bf16[2,4096,384]{2,1,0:T(8,128)(2,1)} %up_hbm.3), custom_call_target="tpu_custom_call" | custom-call | flops 402653184 | bytes 6291456 | tf_op jit(solution)/shard_map/other_gate/pallas_call | solution.py:269
  68.6 3.0 %other_down.1 = bf16[32,64,128]{2,1,0:T(8,128)(2,1)} custom-call(bf16[64,384]{1,0:T(8,128)(2,1)S(1)} %other_gate.1.activation_ref, bf16[64,4096]{1,0:T(8,128)(2,1)S(1)} %collective-permute-done.1.moved_ref, f32[2,64,1]{2,1,0:T(8,128)S(1)} %copy.18.share_ref, bf16[2,384,4096]{2,1,0:T(8,128)(2,1)} %down_hbm.3), custom_call_target="tpu_custom_call" | custom-call | flops 201326592 | bytes 3145728 | tf_op jit(solution)/shard_map/other_down/pallas_call | solution.py:269
  71.7 4.2 %all-to-all-start.2 = ((bf16[32,64,128]{2,1,0:T(8,128)(2,1)}), bf16[32,64,128]{2,1,0:T(8,128)(2,1)S(1)}, u32[]{:S(2)}, u32[]{:S(2)}) async-start(bf16[32,64,128]{2,1,0:T(8,128)(2,1)} %other_down.1), calls=%async_computation.2 | async-start | bytes 1048576 | tf_op jit(solution)/shard_map/all_to_all | solution.py:287
  75.9 11.8 %all-to-all-done.2 = bf16[32,64,128]{2,1,0:T(8,128)(2,1)S(1)} async-done(((bf16[32,64,128]{2,1,0:T(8,128)(2,1)}), bf16[32,64,128]{2,1,0:T(8,128)(2,1)S(1)}, u32[]{:S(2)}, u32[]{:S(2)}) %all-to-all-start.2) | async-done | bytes 524320 | tf_op jit(solution)/shard_map/all_to_all | solution.py:287
  87.6 0.7 fusion.3
  88.4 8.2 %all-gather.1 = f32[1024,128]{1,0:T(8,128)S(1)} all-gather(f32[256,128]{1,0:T(8,128)S(1)} %fusion.3), channel_id=3, replica_groups=mesh['sec'=4,'dev'=32] {'sec'}, dimensions={0}, use_global_device_ids=true | all-gather | bytes 655360 | tf_op jit(solution)/shard_map/all_gather | solution.py:388
  96.6 0.7 add_convert_fusion
  (19 shorter events, 0.2 us)
Async XLA Ops:
  0.0 32.9 %copy-start = (bf16[2048,128]{1,0:T(8,128)(2,1)S(1)}, bf16[2048,128]{1,0:T(8,128)(2,1)}, u32[]{:S(2)}) copy-start(bf16[2048,128]{1,0:T(8,128)(2,1)} %param.17) | copy-start | bytes 1572868
  6.2 9.3 %copy-start.2 = (s32[256,8]{0,1:T(8,128)S(1)}, s32[256,8]{0,1:T(8,128)}, u32[]{:S(2)}) copy-start(s32[256,8]{0,1:T(8,128)} %param.19) | copy-start | bytes 24580
  6.2 26.7 %all-to-all-start = ((bf16[32,8,2176]{2,1,0:T(8,128)(2,1)}), bf16[32,8,2176]{2,1,0:T(8,128)(2,1)S(1)}, u32[]{:S(2)}, u32[]{:S(2)}) async-start(bf16[32,8,2176]{2,1,0:T(8,128)(2,1)} %attend.1), calls=%async_computation | async-start | bytes 2228224 | tf_op jit(solution)/shard_map/all_to_all | solution.py:287
  15.5 26.5 %copy-start.1 = (bf16[256,128]{1,0:T(8,128)(2,1)S(1)}, bf16[256,128]{1,0:T(8,128)(2,1)}, u32[]{:S(2)}) copy-start(bf16[256,128]{1,0:T(8,128)(2,1)} %param.16) | copy-start | bytes 196612
  33.3 14.7 %copy-start.3 = (f32[256,8]{0,1:T(8,128)S(1)}, f32[256,8]{0,1:T(8,128)}, u32[]{:S(2)}) copy-start(f32[256,8]{0,1:T(8,128)} %param.20) | copy-start | bytes 24580
  43.2 16.9 %all-to-all-start.1 = ((bf16[32,64,128]{2,1,0:T(8,128)(2,1)}), bf16[32,64,128]{2,1,0:T(8,128)(2,1)S(1)}, u32[]{:S(2)}, u32[]{:S(2)}) async-start(bf16[32,64,128]{2,1,0:T(8,128)(2,1)} %fusion.2), calls=%async_computation.1 | async-start | bytes 1048576 | tf_op jit(solution)/shard_map/all_to_all | solution.py:287
  60.1 5.1 %collective-permute-start = (bf16[32,64,128]{2,1,0:T(8,128)(2,1)S(1)}, bf16[32,64,128]{2,1,0:T(8,128)(2,1)S(1)}, u32[]{:S(2)}, u32[]{:S(2)}) collective-permute-start(bf16[32,64,128]{2,1,0:T(8,128)(2,1)S(1)} %all-to-all-done.1.rows_ref), channel_id=1, source_target_pairs={{0,32},{32,0},{64,96},{96,64},{1,33},{33,1},{65,97},{97,65},{2,34}... | collective-permute-start | bytes 1572872 | tf_op jit(solution)/shard_map/ppermute | solution.py:338
  64.7 4.0 %collective-permute-start.1 = (bf16[64,4096]{1,0:T(8,128)(2,1)S(1)}, bf16[64,4096]{1,0:T(8,128)(2,1)S(1)}, u32[]{:S(2)}, u32[]{:S(2)}) collective-permute-start(bf16[64,4096]{1,0:T(8,128)(2,1)S(1)} %own_expert.1), channel_id=1, source_target_pairs={{0,32},{32,0},{64,96},{96,64},{1,33},{33,1},{65,97},{97,65},{2,34}... | collective-permute-start | bytes 1572872 | tf_op jit(solution)/shard_map/ppermute | solution.py:367
  71.7 16.0 %all-to-all-start.2 = ((bf16[32,64,128]{2,1,0:T(8,128)(2,1)}), bf16[32,64,128]{2,1,0:T(8,128)(2,1)S(1)}, u32[]{:S(2)}, u32[]{:S(2)}) async-start(bf16[32,64,128]{2,1,0:T(8,128)(2,1)} %other_down.1), calls=%async_computation.2 | async-start | bytes 1048576 | tf_op jit(solution)/shard_map/all_to_all | solution.py:287

commit v3 on v2

--- a/solution.py
+++ b/solution.py
@@ -2,6 +2,7 @@
 
 import jax
 import jax.numpy as jnp
+import numpy as np
 from jax import lax
 from jax.experimental import pallas as pl
 from jax.experimental.pallas import tpu as pltpu
@@ -13,8 +14,13 @@
 HEAD_SIZE = 128
 CAP = 64
 GROUPS = 32
+PLANE = 16
 CHUNKS = 4
-CORE_SWAP = [(0, 1), (1, 0), (2, 3), (3, 2)]
+ROW_GROUP = 4
+AXES = {"y_hi": 2, "core": 2, "z": 4, "y_lo": 2, "x": 4}
+SEC = ("y_hi", "core")
+DEV = ("z", "y_lo", "x")
+SWAP = [(0, 1), (1, 0)]
 
 
 def attend_kernel(
@@ -61,7 +67,7 @@
             )
         )
     ]
-    for copy in small_copies + key_copies + value_copies:
+    for copy in small_copies + [c for pair in zip(key_copies, value_copies) for c in pair]:
         copy.start()
     for copy in small_copies:
         copy.wait()
@@ -78,17 +84,18 @@
         head_queries[pl.ds(h, rows, stride=heads), :] = queries_ref[
             :, h * HEAD_SIZE : (h + 1) * HEAD_SIZE
         ].astype(jnp.float32)
-    for r in range(rows):
-        key_copies[r].wait()
-        head_scores[r * heads : (r + 1) * heads, :] = lax.dot_general(
+    slot = lax.broadcasted_iota(jnp.int32, (heads, slots), 1)
+    pending = {}
+
+    def score(r):
+        return lax.dot_general(
             head_queries[r * heads : (r + 1) * heads, :].astype(jnp.bfloat16),
             keys[r],
             (((1,), (1,)), ((), ())),
             preferred_element_type=jnp.float32,
         )
-    slot = lax.broadcasted_iota(jnp.int32, (heads, slots), 1)
-    weights, own_weights, normalizers = [], [], []
-    for r in range(rows):
+
+    def weigh(r, scores):
         own_key = fresh_ref[0, r : r + 1, :].astype(jnp.float32)
         own_score = (
             jnp.sum(
@@ -96,22 +103,39 @@
             )
             * scale
         )
-        scores = jnp.where(
-            slot < lengths_ref[r], head_scores[r * heads : (r + 1) * heads, :] * scale, -jnp.inf
-        )
+        scores = jnp.where(slot < lengths_ref[r], scores * scale, -jnp.inf)
         row_max = jnp.maximum(jnp.max(scores, axis=1, keepdims=True), own_score)
         weight = jnp.exp(scores - row_max)
         own_weight = jnp.exp(own_score - row_max)
-        normalizers.append(jnp.sum(weight, axis=1, keepdims=True) + own_weight)
-        weights.append(weight.astype(jnp.bfloat16))
-        own_weights.append(own_weight)
-    for r in range(rows):
-        value_copies[r].wait()
+        normalizer = jnp.sum(weight, axis=1, keepdims=True) + own_weight
+        return weight.astype(jnp.bfloat16), own_weight, normalizer
+
+    def blend(r, weight, own_weight, normalizer):
         own_value = fresh_ref[1, r : r + 1, :].astype(jnp.float32)
-        weighted = jnp.dot(weights[r], values[r], preferred_element_type=jnp.float32)
+        weighted = jnp.dot(weight, values[r], preferred_element_type=jnp.float32)
         head_outputs[r * heads : (r + 1) * heads, :] = (
-            weighted + own_weights[r] * own_value
-        ) / normalizers[r]
+            weighted + own_weight * own_value
+        ) / normalizer
+
+    scored, weighed = {}, {}
+    groups = rows // ROW_GROUP
+    members = lambda g: range(g * ROW_GROUP, (g + 1) * ROW_GROUP)
+    for g in range(groups + 2):
+        if g < groups:
+            for r in members(g):
+                key_copies[r].wait()
+        if g >= 2:
+            for r in members(g - 2):
+                value_copies[r].wait()
+        if g < groups:
+            for r in members(g):
+                scored[r] = score(r)
+        if 1 <= g <= groups:
+            for r in members(g - 1):
+                weighed[r] = weigh(r, scored.pop(r))
+        if g >= 2:
+            for r in members(g - 2):
+                blend(r, *weighed.pop(r))
     for h in range(heads):
         staged[:, h * HEAD_SIZE : (h + 1) * HEAD_SIZE] = head_outputs[
             pl.ds(h, rows, stride=heads), :
@@ -133,7 +157,7 @@
     operands = (lengths, queries, fresh_key_value, norm_gain.reshape(1, HEAD_SIZE), key_value_cache)
     return pl.pallas_call(
         attend_kernel,
-        out_shape=jax.ShapeDtypeStruct((GROUPS, rows, width + HEAD_SIZE), jnp.bfloat16),
+        out_shape=jax.ShapeDtypeStruct((PLANE, rows, width + HEAD_SIZE), jnp.bfloat16),
         in_specs=[pl.BlockSpec(memory_space=pl.ANY)] * len(operands),
         out_specs=pl.BlockSpec(memory_space=pl.ANY),
         scratch_shapes=[
@@ -150,7 +174,7 @@
             pltpu.SemaphoreType.DMA((4,)),
             pltpu.SemaphoreType.DMA((rows,)),
             pltpu.SemaphoreType.DMA((rows,)),
-            pltpu.SemaphoreType.DMA((GROUPS,)),
+            pltpu.SemaphoreType.DMA((PLANE,)),
         ],
         compiler_params=pltpu.CompilerParams(vmem_limit_bytes=12 << 20),
         cost_estimate=pl.CostEstimate(
@@ -210,16 +234,29 @@
 
 
 def own_expert_kernel(
-    rows_ref, gain_ref, share_ref, gate_hbm, up_hbm, down_hbm, out_ref, picked, gate, up, down, sems
+    rows_ref,
+    gain_ref,
+    share_ref,
+    gate_hbm,
+    up_hbm,
+    down_hbm,
+    out_ref,
+    next_down,
+    picked,
+    gate,
+    up,
+    down,
+    sems,
 ):
-    expert = lax.rem(lax.axis_index("sec"), 2)
+    expert = lax.axis_index("core")
     gate_copies = row_copies(gate_hbm, expert, gate, sems.at[0])
     up_copies = row_copies(up_hbm, expert, up, sems.at[1])
     down_copies = column_copies(down_hbm, expert, down, sems.at[2])
+    next_copies = column_copies(down_hbm, 1 - expert, next_down, sems.at[3])
     for gate_copy, up_copy in zip(gate_copies, up_copies):
         gate_copy.start()
         up_copy.start()
-    for copy in down_copies:
+    for copy in down_copies + next_copies:
         copy.start()
     fill_picked(rows_ref, gain_ref, picked)
     activation = activate(picked, gate, gate_copies, up, up_copies)
@@ -229,10 +266,12 @@
         copy.wait()
         part = jnp.dot(activation, down[k], preferred_element_type=jnp.float32)
         out_ref[:, k * step : (k + 1) * step] = (part * share).astype(jnp.bfloat16)
+    for copy in next_copies:
+        copy.wait()
 
 
 def other_gate_kernel(rows_ref, gain_ref, gate_hbm, up_hbm, out_ref, picked, gate, up, sems):
-    expert = 1 - lax.rem(lax.axis_index("sec"), 2)
+    expert = 1 - lax.axis_index("core")
     gate_copies = row_copies(gate_hbm, expert, gate, sems.at[0])
     up_copies = row_copies(up_hbm, expert, up, sems.at[1])
     for gate_copy, up_copy in zip(gate_copies, up_copies):
@@ -242,36 +281,37 @@
     out_ref[...] = activate(picked, gate, gate_copies, up, up_copies)
 
 
-def other_down_kernel(activation_ref, moved_ref, share_ref, down_hbm, out_ref, down, sems):
-    expert = 1 - lax.rem(lax.axis_index("sec"), 2)
-    down_copies = column_copies(down_hbm, expert, down, sems.at[0])
-    for copy in down_copies:
-        copy.start()
+def other_down_kernel(activation_ref, moved_ref, share_ref, down, out_hbm, staged, sems):
+    expert = 1 - lax.axis_index("core")
     share = share_ref[expert]
     activation = activation_ref[...]
-    width = out_ref.shape[2]
+    width = staged.shape[2]
     step = down.shape[2]
-    for k, copy in enumerate(down_copies):
-        copy.wait()
+    groups = step // width
+    copies = []
+    for k in range(down.shape[0]):
         part = jnp.dot(activation, down[k], preferred_element_type=jnp.float32)
         part = part * share + moved_ref[:, k * step : (k + 1) * step].astype(jnp.float32)
-        for g in range(step // width):
-            out_ref[k * step // width + g] = part[:, g * width : (g + 1) * width].astype(
-                jnp.bfloat16
-            )
-
-
-def expert_call(kernel, name, out_shape, scratch, small, weights):
+        for g in range(groups):
+            staged[k * groups + g] = part[:, g * width : (g + 1) * width].astype(jnp.bfloat16)
+        place = pl.ds(k * groups, groups)
+        copies.append(pltpu.make_async_copy(staged.at[place], out_hbm.at[place], sems.at[0, k]))
+        copies[-1].start()
+    for copy in copies:
+        copy.wait()
+
+
+def expert_call(kernel, name, outs, scratch, small, weights):
     vmem = pl.BlockSpec(memory_space=pltpu.VMEM)
     any_space = pl.BlockSpec(memory_space=pl.ANY)
     size = sum(weight.size // 2 for weight in weights)
-    sems = pltpu.SemaphoreType.DMA((len(weights), CHUNKS))
     return pl.pallas_call(
         kernel,
-        out_shape=jax.ShapeDtypeStruct(out_shape, jnp.bfloat16),
+        out_shape=[space(shape, jnp.bfloat16) for space, shape in outs],
         in_specs=[vmem] * len(small) + [any_space] * len(weights),
-        out_specs=vmem,
-        scratch_shapes=[pltpu.VMEM(shape, jnp.bfloat16) for shape in scratch] + [sems],
+        out_specs=[vmem if space is pltpu.VMEM else any_space for space, _ in outs],
+        scratch_shapes=[pltpu.VMEM(shape, jnp.bfloat16) for shape in scratch]
+        + [pltpu.SemaphoreType.DMA((4, CHUNKS))],
         compiler_params=pltpu.CompilerParams(vmem_limit_bytes=20 << 20),
         cost_estimate=pl.CostEstimate(
             flops=2 * CAP * size, bytes_accessed=2 * size, transcendentals=0
@@ -283,8 +323,88 @@
     )
 
 
-def exchange(blocks):
-    return lax.all_to_all(blocks, "dev", 0, 0, tiled=True)
+def exchange(blocks, axes):
+    return lax.all_to_all(blocks, axes, 0, 0, tiled=True)
+
+
+def project_kernel(gathered_ref, own_ref, pair_ref, out_ref):
+    half = lax.axis_index("y_lo")
+    rows, width = out_ref.shape[1], own_ref.shape[0]
+    attn = gathered_ref[:, :, :width].reshape(rows, width)
+    own = jnp.dot(attn, own_ref[...], preferred_element_type=jnp.float32).astype(jnp.bfloat16)
+    pair = jnp.dot(attn, pair_ref[...], preferred_element_type=jnp.float32).astype(jnp.bfloat16)
+    for s in range(out_ref.shape[0] // 2):
+        out_ref[2 * s + half] = own
+        out_ref[2 * s + 1 - half] = pair
+
+
+def project(gathered, own, pair):
+    vmem = pl.BlockSpec(memory_space=pltpu.VMEM)
+    groups, rows, _ = gathered.shape
+    width, features = own.shape
+    return pl.pallas_call(
+        project_kernel,
+        out_shape=jax.ShapeDtypeStruct((8, groups * rows, features), jnp.bfloat16),
+        in_specs=[vmem] * 3,
+        out_specs=vmem,
+        compiler_params=pltpu.CompilerParams(vmem_limit_bytes=8 << 20),
+        cost_estimate=pl.CostEstimate(
+            flops=4 * groups * rows * own.size, bytes_accessed=2 << 20, transcendentals=0
+        ),
+        name="project",
+    )(gathered, own, pair)
+
+
+def dispatch_kernel(parts_ref, residual_ref, ranks_ref, hidden_ref, sent_ref, mask):
+    rows, features = residual_ref.shape
+    span = parts_ref.shape[1] // AXES["z"]
+    for z in range(AXES["z"]):
+        for half in range(2):
+            place = (2 * z + half) * span
+            total = residual_ref[place : place + span, :].astype(jnp.float32)
+            for s in range(4):
+                part = parts_ref[2 * s + half, z * span : (z + 1) * span, :]
+                total = total + part.astype(jnp.float32)
+            hidden_ref[place : place + span, :] = total
+    slot = lax.broadcasted_iota(jnp.int32, (CAP, rows), 0)
+    for e in range(GROUPS):
+        mask[e * CAP : (e + 1) * CAP, :] = jnp.where(
+            ranks_ref[e : e + 1, :] == slot, 1.0, 0.0
+        ).astype(jnp.bfloat16)
+    hidden = hidden_ref[...].astype(jnp.bfloat16)
+    step = 8
+    for e in range(0, GROUPS, step):
+        picked = jnp.dot(
+            mask[e * CAP : (e + step) * CAP, :], hidden, preferred_element_type=jnp.float32
+        ).astype(jnp.bfloat16)
+        for i in range(step):
+            sent_ref[e + i] = picked[i * CAP : (i + 1) * CAP, :]
+
+
+def dispatch(parts, residual, ranks):
+    vmem = pl.BlockSpec(memory_space=pltpu.VMEM)
+    rows, features = residual.shape
+    return pl.pallas_call(
+        dispatch_kernel,
+        out_shape=[
+            jax.ShapeDtypeStruct((rows, features), jnp.float32),
+            jax.ShapeDtypeStruct((GROUPS, CAP, features), jnp.bfloat16),
+        ],
+        in_specs=[vmem] * 3,
+        out_specs=[vmem] * 2,
+        scratch_shapes=[pltpu.VMEM((GROUPS * CAP, rows), jnp.bfloat16)],
+        compiler_params=pltpu.CompilerParams(vmem_limit_bytes=8 << 20),
+        cost_estimate=pl.CostEstimate(
+            flops=2 * GROUPS * CAP * rows * features, bytes_accessed=2 << 20, transcendentals=0
+        ),
+        name="dispatch",
+    )(parts, residual, ranks)
+
+
+def sum_over_sec(part):
+    pair = part + lax.ppermute(part, "core", SWAP)
+    pair = pair.astype(jnp.bfloat16)
+    return pair.astype(jnp.float32) + lax.ppermute(pair, "y_hi", SWAP).astype(jnp.float32)
 
 
 def slot_tables(routes):
@@ -316,26 +436,25 @@
 ):
     row_count = routes.shape[0]
     width = queries.shape[1]
-    core = lax.axis_index("sec") % 2
-    group = lax.axis_index("dev")
+    core = lax.axis_index("core")
+    half = lax.axis_index("y_lo")
+    group = lax.axis_index(DEV)
+    pair_weight = lax.ppermute(out_weight, "y_lo", SWAP)
     blocks = attend(queries, fresh_key_value, key_value_cache, lengths, norm_gain)
-    gathered = exchange(blocks)
-    gain = jnp.sum(gathered[:, :3, width:].astype(jnp.float32), axis=1)
-    partial_out = jnp.dot(
-        gathered[:, :, :width].reshape(row_count, width),
-        out_weight,
-        preferred_element_type=jnp.float32,
-    )
-    hidden = residual.astype(jnp.float32) + jnp.sum(lax.all_gather(partial_out, "sec"), axis=0)
+    gathered = exchange(blocks, ("z", "x"))
+    parts = exchange(project(gathered, out_weight, pair_weight), ("y_hi", "core", "y_lo"))
+    own_gain = jnp.sum(gathered[:, :3, width:].astype(jnp.float32), axis=1)
+    pair_gain = lax.ppermute(own_gain, "y_lo", SWAP)
+    gain = jnp.where(half == 0, jnp.stack([own_gain, pair_gain]), jnp.stack([pair_gain, own_gain]))
+    gain = gain.reshape(2, AXES["z"], AXES["x"], HEAD_SIZE).transpose(1, 0, 2, 3)
+    gain = gain.reshape(GROUPS, HEAD_SIZE)
 
     ranks = slot_tables(routes).reshape(GROUPS, 2, row_count)
     own_ranks = lax.dynamic_index_in_dim(ranks, core, 1, keepdims=False)
     other_ranks = lax.dynamic_index_in_dim(ranks, 1 - core, 1, keepdims=False)
-    sent = jnp.einsum(
-        "ekr,rf->ekf", one_hot(own_ranks), hidden.astype(jnp.bfloat16), preferred_element_type=jnp.float32
-    ).astype(jnp.bfloat16)
-    own_rows = exchange(sent)
-    other_rows = lax.ppermute(own_rows, "sec", CORE_SWAP)
+    hidden, sent = dispatch(parts, residual, own_ranks)
+    own_rows = exchange(sent, DEV)
+    other_rows = lax.ppermute(own_rows, "core", SWAP)
 
     local_ids = 2 * group + jnp.arange(2, dtype=jnp.int32)
     local_ranks = lax.dynamic_index_in_dim(ranks, group, 0, keepdims=False)
@@ -356,57 +475,61 @@
     picked_shape = (CAP, D)
     gate_shape = (CHUNKS, D // CHUNKS, units)
     down_shape = (CHUNKS, units, D // CHUNKS)
-    own_result = expert_call(
+    own_result, next_down = expert_call(
         own_expert_kernel,
         "own_expert",
-        (CAP, D),
+        [(pltpu.VMEM, (CAP, D)), (pltpu.VMEM, down_shape)],
         [picked_shape, gate_shape, gate_shape, down_shape],
         [own_rows, gain, share],
         [w_gate, w_up, w_down],
     )
-    moved = lax.ppermute(own_result, "sec", CORE_SWAP)
-    activation = expert_call(
+    moved = lax.ppermute(own_result, "core", SWAP)
+    (activation,) = expert_call(
         other_gate_kernel,
         "other_gate",
-        (CAP, units),
+        [(pltpu.VMEM, (CAP, units))],
         [picked_shape, gate_shape, gate_shape],
         [other_rows, gain],
         [w_gate, w_up],
     )
-    summed = expert_call(
+    out_shape = (GROUPS, CAP, D // GROUPS)
+    (summed,) = expert_call(
         other_down_kernel,
         "other_down",
-        (GROUPS, CAP, D // GROUPS),
-        [down_shape],
-        [activation, moved, share],
-        [w_down],
-    )
-    returned = exchange(summed)
+        [(pltpu.HBM, out_shape)],
+        [out_shape],
+        [activation, moved, share, next_down],
+        [],
+    )
+    returned = exchange(summed, DEV)
     mixture_part = jnp.einsum(
         "ekr,ekf->rf", one_hot(other_ranks), returned, preferred_element_type=jnp.float32
     )
-    mixture = jnp.sum(lax.all_gather(mixture_part, "sec"), axis=0)
+    mixture = sum_over_sec(mixture_part)
     return (hidden + mixture).astype(jnp.bfloat16)
 
 
 def solution(mesh):
+    named = jax.sharding.Mesh(
+        np.reshape(mesh.devices, tuple(AXES.values())), tuple(AXES)
+    )
     return jax.shard_map(
         shards,
-        mesh=mesh,
+        mesh=named,
         in_specs=(
-            P("dev", "sec"),
-            P(None, "dev", "sec"),
-            P(None, "dev", None, "sec"),
-            P("dev"),
-            P(None, "dev"),
-            P("sec", "dev"),
-            P("dev"),
+            P(DEV, SEC),
+            P(None, DEV, SEC),
+            P(None, DEV, None, SEC),
+            P(DEV),
+            P(None, DEV),
+            P(SEC, DEV),
+            P(DEV),
             P(),
             P(),
-            P("dev", None, "sec"),
-            P("dev", None, "sec"),
-            P("dev", "sec", None),
+            P(DEV, None, SEC),
+            P(DEV, None, SEC),
+            P(DEV, SEC, None),
         ),
-        out_specs=P(None, "dev"),
+        out_specs=P(None, DEV),
         check_vma=False,
     )

time: 99 us -> 90.3 us (0.912); the launches traced: 97.2 us -> 89.8 us
  blocking collectives: 16.8 us -> 0 us
  starting transfers between devices: 18.8 us -> 25.7 us
  waiting for transfers between devices: 40.4 us -> 45.4 us
  matrix products: 2.67 us -> 0.98 us
    all_gather x2 -> x0, blocking collectives: 16.8 us -> none  [the longest x1 8.58 us: shards(): lax.all_gather(partial_out, 'sec')]
    ppermute x2 -> x6, waiting for transfers between devices: 0.01 us -> 8.82 us  [the longest x1 4.42 us: sum_over_sec(): lax.ppermute(pair, 'y_hi', SWAP).astype(jnp.float32)]
    ppermute x2 -> x6, starting transfers between devices: 0.59 us -> 5.53 us  [the longest x1 1.78 us: shards(): pair_gain = lax.ppermute(own_gain, 'y_lo', SWAP)]
    all_to_all x3 -> x4, waiting for transfers between devices: 40.4 us -> 36.6 us  [exchange(): return lax.all_to_all(blocks, axes, 0, 0, tiled=True)]
    all_to_all x3 -> x4, starting transfers between devices: 18.2 us -> 20.2 us  [exchange(): return lax.all_to_all(blocks, axes, 0, 0, tiled=True)]
    dot_general x2 -> x0, matrix products: 1.69 us -> none  [the longest x1 1.26 us: shards(): jnp.einsum('ekr,rf->ekf', one_hot(own_ranks), hidden.astype(jnp.bfloat16)...]
    pallas_call x4 -> x6, Pallas kernels: 17.1 us -> 16.3 us  [the longest x3 9.67 us: expert_call(): pl.pallas_call(kernel, out_shape=[space(shape, jnp.bfloat16) for space, s...]
  transfers between devices with their start and end apart: 5 -> 10, of which waited for: 3 -> 7; matrix products, arithmetic and copies ran while one was open for 1% -> 1% of each run, Pallas kernels for 8% -> 14%
where the time goes in v3:
time: 90.3 us; the launch traced here: 89.8 us
  waiting for transfers between devices  45.4 us (50%)
  starting transfers between devices  25.7 us (28%)
  Pallas kernels  16.3 us (18%)
  matrix products  0.98 us (1%)
  other arithmetic  0.97 us (1%)
    all_to_all x4, waiting for transfers between devices, exchange(): return lax.all_to_all(blocks, axes, 0, 0, tiled=True)  36.6 us
    all_to_all x4, starting transfers between devices, exchange(): return lax.all_to_all(blocks, axes, 0, 0, tiled=True)  20.2 us
    pallas_call x3, Pallas kernels, expert_call(): pl.pallas_call(kernel, out_shape=[space(shape, jnp.bfloat16) for space, s...  9.67 us
    ppermute x1, waiting for transfers between devices, sum_over_sec(): lax.ppermute(pair, 'y_hi', SWAP).astype(jnp.float32)  4.42 us
    pallas_call x1, Pallas kernels, attend(): pl.pallas_call(attend_kernel, out_shape=jax.ShapeDtypeStruct((PLANE, rows...  4.29 us
    ppermute x1, waiting for transfers between devices, shards(): pair_gain = lax.ppermute(own_gain, 'y_lo', SWAP)  3.05 us
  transfers between devices with their start and end apart: 10, of which 7 were waited for; matrix products, arithmetic and copies ran while one was open for 1% of the time, Pallas kernels for 14%

profile of v3, /device:TPU:0, one launch (start us, length us, event | category | flops | bytes accessed | tf_op | source)
XLA Modules:
  0.0 89.8 jit_solution(2123265860464022468)
XLA Ops:
  0.0 1.7 %collective-permute-start = (bf16[2048,128]{1,0:T(8,128)(2,1)}, bf16[2048,128]{1,0:T(8,128)(2,1)S(1)}, u32[]{:S(2)}, u32[]{:S(2)}) collective-permute-start(bf16[2048,128]{1,0:T(8,128)(2,1)} %own_ref.1), channel_id=1, source_target_pairs={{0,4},{4,0},{1,5},{5,1},{2,6},{6,2},{3,7},{7,3},{8,12},{12,8},{9,1... | collective-permute-start | bytes 1572872 | tf_op jit(solution)/shard_map/ppermute | solution.py:442
  1.7 4.3 %attend.1 = bf16[16,8,2176]{2,1,0:T(8,128)(2,1)} custom-call(s32[8]{0:T(128)} %lengths_hbm.1, bf16[8,2048]{1,0:T(8,128)(2,1)} %queries_hbm.1, bf16[2,8,128]{2,1,0:T(8,128)(2,1)} %fresh_hbm.1, f32[1,128]{1,0:T(1,128)} %bitcast.28, bf16[2,8,1024,128]{3,2,1,0:T(8,128)(2,1)} %cache_ref.1), custom_call_target="tpu_custom_call" | custom-call | flops 67108864 | bytes 5242880 | tf_op jit(solution)/shard_map/attend/pallas_call | solution.py:158
  6.0 7.9 %all-to-all-start = ((bf16[16,8,2176]{2,1,0:T(8,128)(2,1)}), bf16[16,8,2176]{2,1,0:T(8,128)(2,1)S(1)}, u32[]{:S(2)}, u32[]{:S(2)}) async-start(bf16[16,8,2176]{2,1,0:T(8,128)(2,1)} %attend.1), calls=%async_computation | async-start | bytes 1114112 | tf_op jit(solution)/shard_map/all_to_all | solution.py:327
  14.0 11.5 %all-to-all-done.gathered_ref = bf16[16,8,2176]{2,1,0:T(8,128)(2,1)S(1)} async-done(((bf16[16,8,2176]{2,1,0:T(8,128)(2,1)}), bf16[16,8,2176]{2,1,0:T(8,128)(2,1)S(1)}, u32[]{:S(2)}, u32[]{:S(2)}) %all-to-all-start) | async-done | bytes 557088 | tf_op jit(solution)/shard_map/all_to_all | solution.py:327
  25.5 1.1 %project.1 = bf16[8,128,128]{2,1,0:T(8,128)(2,1)} custom-call(bf16[16,8,2176]{2,1,0:T(8,128)(2,1)S(1)} %all-to-all-done.gathered_ref, bf16[2048,128]{1,0:T(8,128)(2,1)S(1)} %copy-done, bf16[2048,128]{1,0:T(8,128)(2,1)S(1)} %collective-permute-done.pair_ref), custom_call_target="tpu_custom_call" | custom-call | flops 134217728 | bytes 2097152 | tf_op jit(solution)/shard_map/project/pallas_call | solution.py:345
  26.6 4.2 %all-to-all-start.1 = ((bf16[8,128,128]{2,1,0:T(8,128)(2,1)}), bf16[8,128,128]{2,1,0:T(8,128)(2,1)S(1)}, u32[]{:S(2)}, u32[]{:S(2)}) async-start(bf16[8,128,128]{2,1,0:T(8,128)(2,1)} %project.1), calls=%async_computation.1 | async-start | bytes 524288 | tf_op jit(solution)/shard_map/all_to_all | solution.py:327
  30.8 0.3 fusion.2
  31.2 7.1 %all-to-all-done.1.parts_ref = bf16[8,128,128]{2,1,0:T(8,128)(2,1)S(1)} async-done(((bf16[8,128,128]{2,1,0:T(8,128)(2,1)}), bf16[8,128,128]{2,1,0:T(8,128)(2,1)S(1)}, u32[]{:S(2)}, u32[]{:S(2)}) %all-to-all-start.1) | async-done | bytes 262176 | tf_op jit(solution)/shard_map/all_to_all | solution.py:327
  38.3 1.3 %dispatch.1 = (f32[256,128]{1,0:T(8,128)S(1)}, bf16[32,64,128]{2,1,0:T(8,128)(2,1)}) custom-call(bf16[8,128,128]{2,1,0:T(8,128)(2,1)S(1)} %all-to-all-done.1.parts_ref, bf16[256,128]{1,0:T(8,128)(2,1)S(1)} %copy-done.1, s32[32,256]{1,0:T(8,128)S(1)} %bitcast.23), custom_call_target="tpu_custom_call" | custom-call | flops 134217728 | bytes 2097152 | tf_op jit(solution)/shard_map/dispatch/pallas_call | solution.py:387
  39.6 3.9 %all-to-all-start.2 = ((bf16[32,64,128]{2,1,0:T(8,128)(2,1)}), bf16[32,64,128]{2,1,0:T(8,128)(2,1)S(1)}, u32[]{:S(2)}, u32[]{:S(2)}) async-start(bf16[32,64,128]{2,1,0:T(8,128)(2,1)} %get-tuple-element.10), calls=%async_computation.2 | async-start | bytes 1048576 | tf_op jit(solution)/shard_map/all_to_all | solution.py:327
  43.6 1.8 %collective-permute-start.2 = (f32[16,128]{1,0:T(8,128)S(1)}, f32[16,128]{1,0:T(8,128)S(1)}, u32[]{:S(2)}, u32[]{:S(2)}) collective-permute-start(f32[16,128]{1,0:T(8,128)S(1)} %convert_reduce_fusion), channel_id=1, source_target_pairs={{0,4},{4,0},{1,5},{5,1},{2,6},{6,2},{3,7},{7,3},{8,12},{12,8},{9,1... | collective-permute-start | bytes 24584 | tf_op jit(solution)/shard_map/ppermute | solution.py:447
  45.6 3.1 %collective-permute-done.2 = f32[16,128]{1,0:T(8,128)S(1)} collective-permute-done((f32[16,128]{1,0:T(8,128)S(1)}, f32[16,128]{1,0:T(8,128)S(1)}, u32[]{:S(2)}, u32[]{:S(2)}) %collective-permute-start.2) | collective-permute-done | bytes 8224 | tf_op jit(solution)/shard_map/ppermute | solution.py:447
  48.7 6.2 %all-to-all-done.2.rows_ref = bf16[32,64,128]{2,1,0:T(8,128)(2,1)S(1)} async-done(((bf16[32,64,128]{2,1,0:T(8,128)(2,1)}), bf16[32,64,128]{2,1,0:T(8,128)(2,1)S(1)}, u32[]{:S(2)}, u32[]{:S(2)}) %all-to-all-start.2) | async-done | bytes 524320 | tf_op jit(solution)/shard_map/all_to_all | solution.py:327
  54.9 4.8 %own_expert.1 = (bf16[64,4096]{1,0:T(8,128)(2,1)S(1)}, bf16[4,384,1024]{2,1,0:T(8,128)(2,1)S(1)}) custom-call(bf16[32,64,128]{2,1,0:T(8,128)(2,1)S(1)} %all-to-all-done.2.rows_ref, f32[32,128]{1,0:T(8,128)S(1)} %bitcast.21, f32[2,64,1]{2,1,0:T(8,128)S(1)} %copy.20.share_ref, bf16[2,4096,384]{2,1,0:T(8,128)(2,1)} %gate_hbm.3, bf16[2,4096,384]{2,1,0:T(8,128)(2,1)} %up_hbm.3, ...), custom_call_target="tpu_custom_call" | custom-call | flops 603979776 | bytes 9437184 | tf_op jit(solution)/shard_map/own_expert/pallas_call | solution.py:308
  59.6 0.6 collective-permute-start.3
  60.2 3.4 %other_gate.1.activation_ref = bf16[64,384]{1,0:T(8,128)(2,1)S(1)} custom-call(bf16[32,64,128]{2,1,0:T(8,128)(2,1)S(1)} %collective-permute-done.1.rows_ref, f32[32,128]{1,0:T(8,128)S(1)} %bitcast.22, bf16[2,4096,384]{2,1,0:T(8,128)(2,1)} %gate_hbm.3, bf16[2,4096,384]{2,1,0:T(8,128)(2,1)} %up_hbm.3), custom_call_target="tpu_custom_call" | custom-call | flops 402653184 | bytes 6291456 | tf_op jit(solution)/shard_map/other_gate/pallas_call | solution.py:308
  63.6 1.5 %other_down.1 = bf16[32,64,128]{2,1,0:T(8,128)(2,1)} custom-call(bf16[64,384]{1,0:T(8,128)(2,1)S(1)} %other_gate.1.activation_ref, bf16[64,4096]{1,0:T(8,128)(2,1)S(1)} %collective-permute-done.3.moved_ref, f32[2,64,1]{2,1,0:T(8,128)S(1)} %copy.20.share_ref, bf16[4,384,1024]{2,1,0:T(8,128)(2,1)S(1)} %get-tuple-element.12.down), custom_call_target="tpu_custom_call" | custom-call | tf_op jit(solution)/shard_map/other_down/pallas_call | solution.py:308
  65.1 4.2 %all-to-all-start.3 = ((bf16[32,64,128]{2,1,0:T(8,128)(2,1)}), bf16[32,64,128]{2,1,0:T(8,128)(2,1)S(1)}, u32[]{:S(2)}, u32[]{:S(2)}) async-start(bf16[32,64,128]{2,1,0:T(8,128)(2,1)} %other_down.1), calls=%async_computation.3 | async-start | bytes 1048576 | tf_op jit(solution)/shard_map/all_to_all | solution.py:327
  69.4 11.8 %all-to-all-done.3 = bf16[32,64,128]{2,1,0:T(8,128)(2,1)S(1)} async-done(((bf16[32,64,128]{2,1,0:T(8,128)(2,1)}), bf16[32,64,128]{2,1,0:T(8,128)(2,1)S(1)}, u32[]{:S(2)}, u32[]{:S(2)}) %all-to-all-start.3) | async-done | bytes 524320 | tf_op jit(solution)/shard_map/all_to_all | solution.py:327
  81.1 0.7 fusion.1
  82.0 1.3 %collective-permute-done.4 = f32[256,128]{1,0:T(8,128)S(1)} collective-permute-done((f32[256,128]{1,0:T(8,128)S(1)}, f32[256,128]{1,0:T(8,128)S(1)}, u32[]{:S(2)}, u32[]{:S(2)}) %collective-permute-start.4) | collective-permute-done | bytes 131104 | tf_op jit(solution)/shard_map/ppermute | solution.py:405
  83.3 1.4 %collective-permute-start.5 = (bf16[256,128]{1,0:T(8,128)(2,1)S(1)}, bf16[256,128]{1,0:T(8,128)(2,1)S(1)}, u32[]{:S(2)}, u32[]{:S(2)}) collective-permute-start(bf16[256,128]{1,0:T(8,128)(2,1)S(1)} %add_convert_fusion.1), channel_id=1, source_target_pairs={{0,64},{64,0},{1,65},{65,1},{2,66},{66,2},{3,67},{67,3},{4,68},{68... | collective-permute-start | bytes 196616 | tf_op jit(solution)/shard_map/ppermute | solution.py:407
  84.7 4.4 %collective-permute-done.5 = bf16[256,128]{1,0:T(8,128)(2,1)S(1)} collective-permute-done((bf16[256,128]{1,0:T(8,128)(2,1)S(1)}, bf16[256,128]{1,0:T(8,128)(2,1)S(1)}, u32[]{:S(2)}, u32[]{:S(2)}) %collective-permute-start.5) | collective-permute-done | bytes 65568 | tf_op jit(solution)/shard_map/ppermute | solution.py:407
  89.2 0.7 add_convert_fusion
  (27 shorter events, 0.6 us)
Async XLA Ops:
  0.0 25.5 %copy-start = (bf16[2048,128]{1,0:T(8,128)(2,1)S(1)}, bf16[2048,128]{1,0:T(8,128)(2,1)}, u32[]{:S(2)}) copy-start(bf16[2048,128]{1,0:T(8,128)(2,1)} %own_ref.1) | copy-start | bytes 1572868
  0.0 13.9 %copy-start.2 = (s32[256,8]{0,1:T(8,128)S(1)}, s32[256,8]{0,1:T(8,128)}, u32[]{:S(2)}) copy-start(s32[256,8]{0,1:T(8,128)} %param.19) | copy-start | bytes 24580
  0.0 25.5 %collective-permute-start = (bf16[2048,128]{1,0:T(8,128)(2,1)}, bf16[2048,128]{1,0:T(8,128)(2,1)S(1)}, u32[]{:S(2)}, u32[]{:S(2)}) collective-permute-start(bf16[2048,128]{1,0:T(8,128)(2,1)} %own_ref.1), channel_id=1, source_target_pairs={{0,4},{4,0},{1,5},{5,1},{2,6},{6,2},{3,7},{7,3},{8,12},{12,8},{9,1... | collective-permute-start | bytes 1572872 | tf_op jit(solution)/shard_map/ppermute | solution.py:442
  1.7 36.7 %copy-start.1 = (bf16[256,128]{1,0:T(8,128)(2,1)S(1)}, bf16[256,128]{1,0:T(8,128)(2,1)}, u32[]{:S(2)}) copy-start(bf16[256,128]{1,0:T(8,128)(2,1)} %residual_ref.1) | copy-start | bytes 196612
  1.7 41.8 %copy-start.3 = (f32[256,8]{0,1:T(8,128)S(1)}, f32[256,8]{0,1:T(8,128)}, u32[]{:S(2)}) copy-start(f32[256,8]{0,1:T(8,128)} %param.20) | copy-start | bytes 24580
  6.0 19.5 %all-to-all-start = ((bf16[16,8,2176]{2,1,0:T(8,128)(2,1)}), bf16[16,8,2176]{2,1,0:T(8,128)(2,1)S(1)}, u32[]{:S(2)}, u32[]{:S(2)}) async-start(bf16[16,8,2176]{2,1,0:T(8,128)(2,1)} %attend.1), calls=%async_computation | async-start | bytes 1114112 | tf_op jit(solution)/shard_map/all_to_all | solution.py:327
  26.6 11.7 %all-to-all-start.1 = ((bf16[8,128,128]{2,1,0:T(8,128)(2,1)}), bf16[8,128,128]{2,1,0:T(8,128)(2,1)S(1)}, u32[]{:S(2)}, u32[]{:S(2)}) async-start(bf16[8,128,128]{2,1,0:T(8,128)(2,1)} %project.1), calls=%async_computation.1 | async-start | bytes 524288 | tf_op jit(solution)/shard_map/all_to_all | solution.py:327
  39.6 15.3 %all-to-all-start.2 = ((bf16[32,64,128]{2,1,0:T(8,128)(2,1)}), bf16[32,64,128]{2,1,0:T(8,128)(2,1)S(1)}, u32[]{:S(2)}, u32[]{:S(2)}) async-start(bf16[32,64,128]{2,1,0:T(8,128)(2,1)} %get-tuple-element.10), calls=%async_computation.2 | async-start | bytes 1048576 | tf_op jit(solution)/shard_map/all_to_all | solution.py:327
  43.6 5.0 %collective-permute-start.2 = (f32[16,128]{1,0:T(8,128)S(1)}, f32[16,128]{1,0:T(8,128)S(1)}, u32[]{:S(2)}, u32[]{:S(2)}) collective-permute-start(f32[16,128]{1,0:T(8,128)S(1)} %convert_reduce_fusion), channel_id=1, source_target_pairs={{0,4},{4,0},{1,5},{5,1},{2,6},{6,2},{3,7},{7,3},{8,12},{12,8},{9,1... | collective-permute-start | bytes 24584 | tf_op jit(solution)/shard_map/ppermute | solution.py:447
  54.8 5.4 %collective-permute-start.1 = (bf16[32,64,128]{2,1,0:T(8,128)(2,1)S(1)}, bf16[32,64,128]{2,1,0:T(8,128)(2,1)S(1)}, u32[]{:S(2)}, u32[]{:S(2)}) collective-permute-start(bf16[32,64,128]{2,1,0:T(8,128)(2,1)S(1)} %all-to-all-done.2.rows_ref), channel_id=1, source_target_pairs={{0,32},{32,0},{1,33},{33,1},{2,34},{34,2},{3,35},{35,3},{4,36},{36... | collective-permute-start | bytes 1572872 | tf_op jit(solution)/shard_map/ppermute | solution.py:457
  59.6 4.0 %collective-permute-start.3 = (bf16[64,4096]{1,0:T(8,128)(2,1)S(1)}, bf16[64,4096]{1,0:T(8,128)(2,1)S(1)}, u32[]{:S(2)}, u32[]{:S(2)}) collective-permute-start(bf16[64,4096]{1,0:T(8,128)(2,1)S(1)} %get-tuple-element.11), channel_id=1, source_target_pairs={{0,32},{32,0},{1,33},{33,1},{2,34},{34,2},{3,35},{35,3},{4,36},{36... | collective-permute-start | bytes 1572872 | tf_op jit(solution)/shard_map/ppermute | solution.py:486
  65.1 16.0 %all-to-all-start.3 = ((bf16[32,64,128]{2,1,0:T(8,128)(2,1)}), bf16[32,64,128]{2,1,0:T(8,128)(2,1)S(1)}, u32[]{:S(2)}, u32[]{:S(2)}) async-start(bf16[32,64,128]{2,1,0:T(8,128)(2,1)} %other_down.1), calls=%async_computation.3 | async-start | bytes 1048576 | tf_op jit(solution)/shard_map/all_to_all | solution.py:327
  81.9 1.4 %collective-permute-start.4 = (f32[256,128]{1,0:T(8,128)S(1)}, f32[256,128]{1,0:T(8,128)S(1)}, u32[]{:S(2)}, u32[]{:S(2)}) collective-permute-start(f32[256,128]{1,0:T(8,128)S(1)} %fusion.1), channel_id=1, source_target_pairs={{0,32},{32,0},{1,33},{33,1},{2,34},{34,2},{3,35},{35,3},{4,36},{36... | collective-permute-start | bytes 393224 | tf_op jit(solution)/shard_map/ppermute | solution.py:405
  83.3 5.8 %collective-permute-start.5 = (bf16[256,128]{1,0:T(8,128)(2,1)S(1)}, bf16[256,128]{1,0:T(8,128)(2,1)S(1)}, u32[]{:S(2)}, u32[]{:S(2)}) collective-permute-start(bf16[256,128]{1,0:T(8,128)(2,1)S(1)} %add_convert_fusion.1), channel_id=1, source_target_pairs={{0,64},{64,0},{1,65},{65,1},{2,66},{66,2},{3,67},{67,3},{4,68},{68... | collective-permute-start | bytes 196616 | tf_op jit(solution)/shard_map/ppermute | solution.py:407

commit v4 on v3

--- a/solution.py
+++ b/solution.py
@@ -1,3 +1,4 @@
+import functools
 import math
 
 import jax
@@ -15,7 +16,9 @@
 CAP = 64
 GROUPS = 32
 PLANE = 16
-CHUNKS = 4
+GATE_CHUNKS = 4
+FIRST = 1536
+DOWN_CHUNKS = 4
 ROW_GROUP = 4
 AXES = {"y_hi": 2, "core": 2, "z": 4, "y_lo": 2, "x": 4}
 SEC = ("y_hi", "core")
@@ -186,6 +189,19 @@
     )(*(pltpu.with_memory_space_constraint(operand, pltpu.HBM) for operand in operands))
 
 
+def land(copies):
+    for copy in copies:
+        copy.wait()
+        yield
+
+
+def in_order(copies, meanwhile):
+    for copy in copies:
+        copy.start()
+    meanwhile()
+    return land(copies)
+
+
 def fill_picked(rows_ref, gain_ref, picked):
     groups, cap, width = rows_ref.shape
     square = jnp.zeros((cap, width), jnp.float32)
@@ -200,11 +216,11 @@
         ).astype(jnp.bfloat16)
 
 
-def row_copies(source, expert, target, sems):
+def row_copies(source, expert, target, sems, skipped=0):
     count, size = target.shape[0], target.shape[1]
     return [
         pltpu.make_async_copy(
-            source.at[expert, pl.ds(k * size, size)], target.at[k], sems.at[k]
+            source.at[expert, pl.ds(skipped + k * size, size)], target.at[k], sems.at[k]
         )
         for k in range(count)
     ]
@@ -220,23 +236,69 @@
     ]
 
 
-def activate(picked, gate, gate_copies, up, up_copies):
-    size = gate.shape[1]
-    gate_part = jnp.zeros((CAP, gate.shape[2]), jnp.float32)
-    upward = gate_part
-    for k in range(gate.shape[0]):
-        part = picked[:, k * size : (k + 1) * size]
-        gate_copies[k].wait()
-        gate_part = gate_part + jnp.dot(part, gate[k], preferred_element_type=jnp.float32)
-        up_copies[k].wait()
-        upward = upward + jnp.dot(part, up[k], preferred_element_type=jnp.float32)
-    return (gate_part / (1.0 + jnp.exp(-gate_part)) * upward).astype(jnp.bfloat16)
+def activate(picked, gates, ups, landed, skipped):
+    gate_sum = up_sum = None
+    start = 0
+    for k, (gate, up) in enumerate(zip(gates, ups)):
+        part = picked[:, start : start + gate.shape[0]]
+        start += gate.shape[0]
+        if k >= skipped:
+            next(landed)
+        product = jnp.dot(part, gate[...], preferred_element_type=jnp.float32)
+        gate_sum = product if gate_sum is None else gate_sum + product
+        if k >= skipped:
+            next(landed)
+        product = jnp.dot(part, up[...], preferred_element_type=jnp.float32)
+        up_sum = product if up_sum is None else up_sum + product
+    return (gate_sum / (1.0 + jnp.exp(-gate_sum)) * up_sum).astype(jnp.bfloat16)
+
+
+def parts_of(array):
+    return [array.at[k] for k in range(array.shape[0])]
+
+
+def paired(first, second):
+    return [copy for pair in zip(first, second) for copy in pair]
+
+
+def preload_kernel(gate_hbm, up_hbm, gate_ref, up_ref, sems):
+    expert = lax.axis_index("core")
+    place = pl.ds(0, gate_ref.shape[0])
+    copies = [
+        pltpu.make_async_copy(gate_hbm.at[expert, place], gate_ref, sems.at[0]),
+        pltpu.make_async_copy(up_hbm.at[expert, place], up_ref, sems.at[1]),
+    ]
+    for copy in copies:
+        copy.start()
+    for copy in copies:
+        copy.wait()
+
+
+def preload(gate, up, rows):
+    shape = (rows, gate.shape[2])
+    return pl.pallas_call(
+        preload_kernel,
+        out_shape=[pltpu.VMEM(shape, jnp.bfloat16)] * 2,
+        in_specs=[pl.BlockSpec(memory_space=pl.ANY)] * 2,
+        out_specs=[pl.BlockSpec(memory_space=pltpu.VMEM)] * 2,
+        scratch_shapes=[pltpu.SemaphoreType.DMA((2,))],
+        compiler_params=pltpu.CompilerParams(vmem_limit_bytes=1 << 20),
+        cost_estimate=pl.CostEstimate(
+            flops=0, bytes_accessed=8 * rows * gate.shape[2], transcendentals=0
+        ),
+        name="preload",
+    )(
+        pltpu.with_memory_space_constraint(gate, pltpu.HBM),
+        pltpu.with_memory_space_constraint(up, pltpu.HBM),
+    )
 
 
 def own_expert_kernel(
     rows_ref,
     gain_ref,
     share_ref,
+    first_gate,
+    first_up,
     gate_hbm,
     up_hbm,
     down_hbm,
@@ -249,36 +311,36 @@
     sems,
 ):
     expert = lax.axis_index("core")
-    gate_copies = row_copies(gate_hbm, expert, gate, sems.at[0])
-    up_copies = row_copies(up_hbm, expert, up, sems.at[1])
+    skipped = first_gate.shape[0]
+    gate_copies = row_copies(gate_hbm, expert, gate, sems.at[0], skipped)
+    up_copies = row_copies(up_hbm, expert, up, sems.at[1], skipped)
     down_copies = column_copies(down_hbm, expert, down, sems.at[2])
     next_copies = column_copies(down_hbm, 1 - expert, next_down, sems.at[3])
-    for gate_copy, up_copy in zip(gate_copies, up_copies):
-        gate_copy.start()
-        up_copy.start()
-    for copy in down_copies + next_copies:
-        copy.start()
-    fill_picked(rows_ref, gain_ref, picked)
-    activation = activate(picked, gate, gate_copies, up, up_copies)
+    copies = paired(gate_copies, up_copies) + down_copies + next_copies
+    landed = in_order(copies, functools.partial(fill_picked, rows_ref, gain_ref, picked))
+    activation = activate(
+        picked, [first_gate] + parts_of(gate), [first_up] + parts_of(up), landed, 1
+    )
     share = share_ref[expert]
     step = down.shape[2]
-    for k, copy in enumerate(down_copies):
-        copy.wait()
+    for k in range(down.shape[0]):
+        next(landed)
         part = jnp.dot(activation, down[k], preferred_element_type=jnp.float32)
         out_ref[:, k * step : (k + 1) * step] = (part * share).astype(jnp.bfloat16)
-    for copy in next_copies:
-        copy.wait()
+    for _ in landed:
+        pass
 
 
 def other_gate_kernel(rows_ref, gain_ref, gate_hbm, up_hbm, out_ref, picked, gate, up, sems):
     expert = 1 - lax.axis_index("core")
     gate_copies = row_copies(gate_hbm, expert, gate, sems.at[0])
     up_copies = row_copies(up_hbm, expert, up, sems.at[1])
-    for gate_copy, up_copy in zip(gate_copies, up_copies):
-        gate_copy.start()
-        up_copy.start()
-    fill_picked(rows_ref, gain_ref, picked)
-    out_ref[...] = activate(picked, gate, gate_copies, up, up_copies)
+    landed = in_order(
+        paired(gate_copies, up_copies), functools.partial(fill_picked, rows_ref, gain_ref, picked)
+    )
+    out_ref[...] = activate(picked, parts_of(gate), parts_of(up), landed, 0)
+    for _ in landed:
+        pass
 
 
 def other_down_kernel(activation_ref, moved_ref, share_ref, down, out_hbm, staged, sems):
@@ -311,8 +373,8 @@
         in_specs=[vmem] * len(small) + [any_space] * len(weights),
         out_specs=[vmem if space is pltpu.VMEM else any_space for space, _ in outs],
         scratch_shapes=[pltpu.VMEM(shape, jnp.bfloat16) for shape in scratch]
-        + [pltpu.SemaphoreType.DMA((4, CHUNKS))],
-        compiler_params=pltpu.CompilerParams(vmem_limit_bytes=20 << 20),
+        + [pltpu.SemaphoreType.DMA((4, max(GATE_CHUNKS, DOWN_CHUNKS)))],
+        compiler_params=pltpu.CompilerParams(vmem_limit_bytes=16 << 20),
         cost_estimate=pl.CostEstimate(
             flops=2 * CAP * size, bytes_accessed=2 * size, transcendentals=0
         ),
@@ -355,7 +417,9 @@
     )(gathered, own, pair)
 
 
-def dispatch_kernel(parts_ref, residual_ref, ranks_ref, hidden_ref, sent_ref, mask):
+def dispatch_kernel(
+    parts_ref, residual_ref, ranks_ref, hidden_ref, sent_hbm, mask, staged, sems
+):
     rows, features = residual_ref.shape
     span = parts_ref.shape[1] // AXES["z"]
     for z in range(AXES["z"]):
@@ -366,33 +430,43 @@
                 part = parts_ref[2 * s + half, z * span : (z + 1) * span, :]
                 total = total + part.astype(jnp.float32)
             hidden_ref[place : place + span, :] = total
+    hidden = hidden_ref[...].astype(jnp.bfloat16)
     slot = lax.broadcasted_iota(jnp.int32, (CAP, rows), 0)
-    for e in range(GROUPS):
-        mask[e * CAP : (e + 1) * CAP, :] = jnp.where(
-            ranks_ref[e : e + 1, :] == slot, 1.0, 0.0
-        ).astype(jnp.bfloat16)
-    hidden = hidden_ref[...].astype(jnp.bfloat16)
-    step = 8
-    for e in range(0, GROUPS, step):
-        picked = jnp.dot(
-            mask[e * CAP : (e + step) * CAP, :], hidden, preferred_element_type=jnp.float32
-        ).astype(jnp.bfloat16)
+    step = GROUPS // sems.shape[0]
+    copies = []
+    for k in range(sems.shape[0]):
         for i in range(step):
-            sent_ref[e + i] = picked[i * CAP : (i + 1) * CAP, :]
+            e = k * step + i
+            mask[i * CAP : (i + 1) * CAP, :] = jnp.where(
+                ranks_ref[e : e + 1, :] == slot, 1.0, 0.0
+            ).astype(jnp.bfloat16)
+        picked = jnp.dot(mask[...], hidden, preferred_element_type=jnp.float32)
+        for i in range(step):
+            staged[k * step + i] = picked[i * CAP : (i + 1) * CAP, :].astype(jnp.bfloat16)
+        place = pl.ds(k * step, step)
+        copies.append(pltpu.make_async_copy(staged.at[place], sent_hbm.at[place], sems.at[k]))
+        copies[-1].start()
+    for copy in copies:
+        copy.wait()
 
 
 def dispatch(parts, residual, ranks):
     vmem = pl.BlockSpec(memory_space=pltpu.VMEM)
     rows, features = residual.shape
+    pieces = 4
     return pl.pallas_call(
         dispatch_kernel,
         out_shape=[
             jax.ShapeDtypeStruct((rows, features), jnp.float32),
-            jax.ShapeDtypeStruct((GROUPS, CAP, features), jnp.bfloat16),
+            pltpu.HBM((GROUPS, CAP, features), jnp.bfloat16),
         ],
         in_specs=[vmem] * 3,
-        out_specs=[vmem] * 2,
-        scratch_shapes=[pltpu.VMEM((GROUPS * CAP, rows), jnp.bfloat16)],
+        out_specs=[vmem, pl.BlockSpec(memory_space=pl.ANY)],
+        scratch_shapes=[
+            pltpu.VMEM((GROUPS // pieces * CAP, rows), jnp.bfloat16),
+            pltpu.VMEM((GROUPS, CAP, features), jnp.bfloat16),
+            pltpu.SemaphoreType.DMA((pieces,)),
+        ],
         compiler_params=pltpu.CompilerParams(vmem_limit_bytes=8 << 20),
         cost_estimate=pl.CostEstimate(
             flops=2 * GROUPS * CAP * rows * features, bytes_accessed=2 << 20, transcendentals=0
@@ -439,21 +513,25 @@
     core = lax.axis_index("core")
     half = lax.axis_index("y_lo")
     group = lax.axis_index(DEV)
-    pair_weight = lax.ppermute(out_weight, "y_lo", SWAP)
     blocks = attend(queries, fresh_key_value, key_value_cache, lengths, norm_gain)
+    blocks, late_weight = lax.optimization_barrier((blocks, out_weight))
+    pair_weight = lax.ppermute(late_weight, "y_lo", SWAP)
     gathered = exchange(blocks, ("z", "x"))
     parts = exchange(project(gathered, out_weight, pair_weight), ("y_hi", "core", "y_lo"))
     own_gain = jnp.sum(gathered[:, :3, width:].astype(jnp.float32), axis=1)
     pair_gain = lax.ppermute(own_gain, "y_lo", SWAP)
-    gain = jnp.where(half == 0, jnp.stack([own_gain, pair_gain]), jnp.stack([pair_gain, own_gain]))
-    gain = gain.reshape(2, AXES["z"], AXES["x"], HEAD_SIZE).transpose(1, 0, 2, 3)
-    gain = gain.reshape(GROUPS, HEAD_SIZE)
-
     ranks = slot_tables(routes).reshape(GROUPS, 2, row_count)
     own_ranks = lax.dynamic_index_in_dim(ranks, core, 1, keepdims=False)
     other_ranks = lax.dynamic_index_in_dim(ranks, 1 - core, 1, keepdims=False)
     hidden, sent = dispatch(parts, residual, own_ranks)
+    sent, pair_gain, late_gate, late_up = lax.optimization_barrier(
+        (sent, pair_gain, w_gate, w_up)
+    )
+    first_gate, first_up = preload(late_gate, late_up, FIRST)
     own_rows = exchange(sent, DEV)
+    gain = jnp.where(half == 0, jnp.stack([own_gain, pair_gain]), jnp.stack([pair_gain, own_gain]))
+    gain = gain.reshape(2, AXES["z"], AXES["x"], HEAD_SIZE).transpose(1, 0, 2, 3)
+    gain = gain.reshape(GROUPS, HEAD_SIZE)
     other_rows = lax.ppermute(own_rows, "core", SWAP)
 
     local_ids = 2 * group + jnp.arange(2, dtype=jnp.int32)
@@ -473,14 +551,15 @@
     share = slot_share[:, :, None]
     units = w_gate.shape[2]
     picked_shape = (CAP, D)
-    gate_shape = (CHUNKS, D // CHUNKS, units)
-    down_shape = (CHUNKS, units, D // CHUNKS)
+    gate_shape = (GATE_CHUNKS, D // GATE_CHUNKS, units)
+    own_shape = (2, (D - FIRST) // 2, units)
+    down_shape = (DOWN_CHUNKS, units, D // DOWN_CHUNKS)
     own_result, next_down = expert_call(
         own_expert_kernel,
         "own_expert",
         [(pltpu.VMEM, (CAP, D)), (pltpu.VMEM, down_shape)],
-        [picked_shape, gate_shape, gate_shape, down_shape],
-        [own_rows, gain, share],
+        [picked_shape, own_shape, own_shape, down_shape],
+        [own_rows, gain, share, first_gate, first_up],
         [w_gate, w_up, w_down],
     )
     moved = lax.ppermute(own_result, "core", SWAP)

time: 90.3 us -> 89.8 us (level)
  waiting for transfers between devices: 45.4 us -> 43.4 us
  Pallas kernels: 16.3 us -> 17.3 us
    ppermute x1, waiting for transfers between devices: 3.05 us -> 0.01 us  [shards(): pair_gain = lax.ppermute(own_gain, 'y_lo', SWAP)]
    pallas_call x0 -> x1, Pallas kernels: none -> 1.65 us  [preload(): pl.pallas_call(preload_kernel, out_shape=[pltpu.VMEM(shape, jnp.bfloat16)...]
    all_to_all x4, waiting for transfers between devices: 36.6 us -> 37.6 us  [exchange(): return lax.all_to_all(blocks, axes, 0, 0, tiled=True)]
  transfers between devices with their start and end apart: 10 -> 10, of which waited for: 7 -> 6; matrix products, arithmetic and copies ran while one was open for 1% -> 1% of each run, Pallas kernels for 14% -> 12%
where the time goes in v4:
time: 89.8 us; the launch traced here: 89.2 us
  waiting for transfers between devices  43.4 us (48%)
  starting transfers between devices  26.1 us (29%)
  Pallas kernels  17.3 us (19%)
  other arithmetic  0.98 us (1%)
  matrix products  0.98 us (1%)
    all_to_all x4, waiting for transfers between devices, exchange(): return lax.all_to_all(blocks, axes, 0, 0, tiled=True)  37.6 us
    all_to_all x4, starting transfers between devices, exchange(): return lax.all_to_all(blocks, axes, 0, 0, tiled=True)  20.2 us
    pallas_call x3, Pallas kernels, expert_call(): pl.pallas_call(kernel, out_shape=[space(shape, jnp.bfloat16) for space, s...  8.99 us
    ppermute x1, waiting for transfers between devices, sum_over_sec(): lax.ppermute(pair, 'y_hi', SWAP).astype(jnp.float32)  4.39 us
    pallas_call x1, Pallas kernels, attend(): pl.pallas_call(attend_kernel, out_shape=jax.ShapeDtypeStruct((PLANE, rows...  4.3 us
    ppermute x1, starting transfers between devices, shards(): pair_gain = lax.ppermute(own_gain, 'y_lo', SWAP)  2.1 us
  transfers between devices with their start and end apart: 10, of which 6 were waited for; matrix products, arithmetic and copies ran while one was open for 1% of the time, Pallas kernels for 12%

profile of v4, /device:TPU:0, one launch (start us, length us, event | category | flops | bytes accessed | tf_op | source)
XLA Modules:
  0.0 89.2 jit_solution(5764940560658091901)
XLA Ops:
  0.0 4.3 %attend.1 = bf16[16,8,2176]{2,1,0:T(8,128)(2,1)} custom-call(s32[8]{0:T(128)} %lengths_hbm.1, bf16[8,2048]{1,0:T(8,128)(2,1)} %queries_hbm.1, bf16[2,8,128]{2,1,0:T(8,128)(2,1)} %fresh_hbm.1, f32[1,128]{1,0:T(1,128)} %bitcast.28, bf16[2,8,1024,128]{3,2,1,0:T(8,128)(2,1)} %cache_ref.1), custom_call_target="tpu_custom_call" | custom-call | flops 67108864 | bytes 5242880 | tf_op jit(solution)/shard_map/attend/pallas_call | solution.py:161
  4.3 1.7 %collective-permute-start = (bf16[2048,128]{1,0:T(8,128)(2,1)S(1)}, bf16[2048,128]{1,0:T(8,128)(2,1)S(1)}, u32[]{:S(2)}, u32[]{:S(2)}) collective-permute-start(bf16[2048,128]{1,0:T(8,128)(2,1)S(1)} %copy-done), channel_id=1, source_target_pairs={{0,4},{4,0},{1,5},{5,1},{2,6},{6,2},{3,7},{7,3},{8,12},{12,8},{9,1... | collective-permute-start | bytes 1572872 | tf_op jit(solution)/shard_map/ppermute | solution.py:518
  6.1 7.9 %all-to-all-start = ((bf16[16,8,2176]{2,1,0:T(8,128)(2,1)}), bf16[16,8,2176]{2,1,0:T(8,128)(2,1)S(1)}, u32[]{:S(2)}, u32[]{:S(2)}) async-start(bf16[16,8,2176]{2,1,0:T(8,128)(2,1)} %attend.1), calls=%async_computation | async-start | bytes 1114112 | tf_op jit(solution)/shard_map/all_to_all | solution.py:389
  14.1 0.3 fusion.2
  14.3 11.2 %all-to-all-done.gathered_ref = bf16[16,8,2176]{2,1,0:T(8,128)(2,1)S(1)} async-done(((bf16[16,8,2176]{2,1,0:T(8,128)(2,1)}), bf16[16,8,2176]{2,1,0:T(8,128)(2,1)S(1)}, u32[]{:S(2)}, u32[]{:S(2)}) %all-to-all-start) | async-done | bytes 557088 | tf_op jit(solution)/shard_map/all_to_all | solution.py:389
  25.6 1.1 %project.1 = bf16[8,128,128]{2,1,0:T(8,128)(2,1)} custom-call(bf16[16,8,2176]{2,1,0:T(8,128)(2,1)S(1)} %all-to-all-done.gathered_ref, bf16[2048,128]{1,0:T(8,128)(2,1)S(1)} %copy-done, bf16[2048,128]{1,0:T(8,128)(2,1)S(1)} %collective-permute-done.pair_ref), custom_call_target="tpu_custom_call" | custom-call | flops 134217728 | bytes 2097152 | tf_op jit(solution)/shard_map/project/pallas_call | solution.py:407
  26.7 4.2 %all-to-all-start.1 = ((bf16[8,128,128]{2,1,0:T(8,128)(2,1)}), bf16[8,128,128]{2,1,0:T(8,128)(2,1)S(1)}, u32[]{:S(2)}, u32[]{:S(2)}) async-start(bf16[8,128,128]{2,1,0:T(8,128)(2,1)} %project.1), calls=%async_computation.1 | async-start | bytes 524288 | tf_op jit(solution)/shard_map/all_to_all | solution.py:389
  31.1 2.1 %collective-permute-start.1 = (f32[16,128]{1,0:T(8,128)S(1)}, f32[16,128]{1,0:T(8,128)S(1)}, u32[]{:S(2)}, u32[]{:S(2)}) collective-permute-start(f32[16,128]{1,0:T(8,128)S(1)} %convert_reduce_fusion), channel_id=1, source_target_pairs={{0,4},{4,0},{1,5},{5,1},{2,6},{6,2},{3,7},{7,3},{8,12},{12,8},{9,1... | collective-permute-start | bytes 24584 | tf_op jit(solution)/shard_map/ppermute | solution.py:522
  33.2 5.4 %all-to-all-done.1.parts_ref = bf16[8,128,128]{2,1,0:T(8,128)(2,1)S(1)} async-done(((bf16[8,128,128]{2,1,0:T(8,128)(2,1)}), bf16[8,128,128]{2,1,0:T(8,128)(2,1)S(1)}, u32[]{:S(2)}, u32[]{:S(2)}) %all-to-all-start.1) | async-done | bytes 262176 | tf_op jit(solution)/shard_map/all_to_all | solution.py:389
  38.5 1.2 %dispatch.1 = (f32[256,128]{1,0:T(8,128)S(1)}, bf16[32,64,128]{2,1,0:T(8,128)(2,1)}) custom-call(bf16[8,128,128]{2,1,0:T(8,128)(2,1)S(1)} %all-to-all-done.1.parts_ref, bf16[256,128]{1,0:T(8,128)(2,1)S(1)} %copy-done.1, s32[32,256]{1,0:T(8,128)S(1)} %bitcast.23), custom_call_target="tpu_custom_call" | custom-call | flops 134217728 | bytes 2097152 | tf_op jit(solution)/shard_map/dispatch/pallas_call | solution.py:457
  39.7 3.9 %all-to-all-start.2 = ((bf16[32,64,128]{2,1,0:T(8,128)(2,1)}), bf16[32,64,128]{2,1,0:T(8,128)(2,1)S(1)}, u32[]{:S(2)}, u32[]{:S(2)}) async-start(bf16[32,64,128]{2,1,0:T(8,128)(2,1)} %get-tuple-element.21), calls=%async_computation.2 | async-start | bytes 1048576 | tf_op jit(solution)/shard_map/all_to_all | solution.py:389
  44.0 1.7 %preload.1 = (bf16[1536,384]{1,0:T(8,128)(2,1)S(1)}, bf16[1536,384]{1,0:T(8,128)(2,1)S(1)}) custom-call(bf16[2,4096,384]{2,1,0:T(8,128)(2,1)} %gate_hbm.4, bf16[2,4096,384]{2,1,0:T(8,128)(2,1)} %up_hbm.4), custom_call_target="tpu_custom_call" | custom-call | bytes 4718592 | tf_op jit(solution)/shard_map/preload/pallas_call | solution.py:279
  45.7 9.3 %all-to-all-done.2.rows_ref = bf16[32,64,128]{2,1,0:T(8,128)(2,1)S(1)} async-done(((bf16[32,64,128]{2,1,0:T(8,128)(2,1)}), bf16[32,64,128]{2,1,0:T(8,128)(2,1)S(1)}, u32[]{:S(2)}, u32[]{:S(2)}) %all-to-all-start.2) | async-done | bytes 524320 | tf_op jit(solution)/shard_map/all_to_all | solution.py:389
  54.9 4.1 %own_expert.1 = (bf16[64,4096]{1,0:T(8,128)(2,1)S(1)}, bf16[4,384,1024]{2,1,0:T(8,128)(2,1)S(1)}) custom-call(bf16[32,64,128]{2,1,0:T(8,128)(2,1)S(1)} %all-to-all-done.2.rows_ref, f32[32,128]{1,0:T(8,128)S(1)} %bitcast.21, f32[2,64,1]{2,1,0:T(8,128)S(1)} %copy.20.share_ref, bf16[1536,384]{1,0:T(8,128)(2,1)S(1)} %get-tuple-element.25.first_gate, ...), custom_call_target="tpu_custom_call" | custom-call | flops 603979776 | bytes 9437184 | tf_op jit(solution)/shard_map/own_expert/pallas_call | solution.py:370
  59.0 0.6 collective-permute-start.3
  59.6 3.4 %other_gate.1.activation_ref = bf16[64,384]{1,0:T(8,128)(2,1)S(1)} custom-call(bf16[32,64,128]{2,1,0:T(8,128)(2,1)S(1)} %collective-permute-done.2.rows_ref, f32[32,128]{1,0:T(8,128)S(1)} %bitcast.22, bf16[2,4096,384]{2,1,0:T(8,128)(2,1)} %gate_hbm.4, bf16[2,4096,384]{2,1,0:T(8,128)(2,1)} %up_hbm.4), custom_call_target="tpu_custom_call" | custom-call | flops 402653184 | bytes 6291456 | tf_op jit(solution)/shard_map/other_gate/pallas_call | solution.py:370
  63.1 1.5 %other_down.1 = bf16[32,64,128]{2,1,0:T(8,128)(2,1)} custom-call(bf16[64,384]{1,0:T(8,128)(2,1)S(1)} %other_gate.1.activation_ref, bf16[64,4096]{1,0:T(8,128)(2,1)S(1)} %collective-permute-done.3.moved_ref, f32[2,64,1]{2,1,0:T(8,128)S(1)} %copy.20.share_ref, bf16[4,384,1024]{2,1,0:T(8,128)(2,1)S(1)} %get-tuple-element.28.down), custom_call_target="tpu_custom_call" | custom-call | tf_op jit(solution)/shard_map/other_down/pallas_call | solution.py:370
  64.6 4.2 %all-to-all-start.3 = ((bf16[32,64,128]{2,1,0:T(8,128)(2,1)}), bf16[32,64,128]{2,1,0:T(8,128)(2,1)S(1)}, u32[]{:S(2)}, u32[]{:S(2)}) async-start(bf16[32,64,128]{2,1,0:T(8,128)(2,1)} %other_down.1), calls=%async_computation.3 | async-start | bytes 1048576 | tf_op jit(solution)/shard_map/all_to_all | solution.py:389
  68.8 11.8 %all-to-all-done.3 = bf16[32,64,128]{2,1,0:T(8,128)(2,1)S(1)} async-done(((bf16[32,64,128]{2,1,0:T(8,128)(2,1)}), bf16[32,64,128]{2,1,0:T(8,128)(2,1)S(1)}, u32[]{:S(2)}, u32[]{:S(2)}) %all-to-all-start.3) | async-done | bytes 524320 | tf_op jit(solution)/shard_map/all_to_all | solution.py:389
  80.6 0.7 fusion.1
  81.4 1.3 %collective-permute-done.4 = f32[256,128]{1,0:T(8,128)S(1)} collective-permute-done((f32[256,128]{1,0:T(8,128)S(1)}, f32[256,128]{1,0:T(8,128)S(1)}, u32[]{:S(2)}, u32[]{:S(2)}) %collective-permute-start.4) | collective-permute-done | bytes 131104 | tf_op jit(solution)/shard_map/ppermute | solution.py:479
  82.7 1.5 %collective-permute-start.5 = (bf16[256,128]{1,0:T(8,128)(2,1)S(1)}, bf16[256,128]{1,0:T(8,128)(2,1)S(1)}, u32[]{:S(2)}, u32[]{:S(2)}) collective-permute-start(bf16[256,128]{1,0:T(8,128)(2,1)S(1)} %add_convert_fusion.1), channel_id=1, source_target_pairs={{0,64},{64,0},{1,65},{65,1},{2,66},{66,2},{3,67},{67,3},{4,68},{68... | collective-permute-start | bytes 196616 | tf_op jit(solution)/shard_map/ppermute | solution.py:481
  84.2 4.4 %collective-permute-done.5 = bf16[256,128]{1,0:T(8,128)(2,1)S(1)} collective-permute-done((bf16[256,128]{1,0:T(8,128)(2,1)S(1)}, bf16[256,128]{1,0:T(8,128)(2,1)S(1)}, u32[]{:S(2)}, u32[]{:S(2)}) %collective-permute-start.5) | collective-permute-done | bytes 65568 | tf_op jit(solution)/shard_map/ppermute | solution.py:481
  88.6 0.7 add_convert_fusion
  (28 shorter events, 0.7 us)
Async XLA Ops:
  0.0 4.3 %copy-start = (bf16[2048,128]{1,0:T(8,128)(2,1)S(1)}, bf16[2048,128]{1,0:T(8,128)(2,1)}, u32[]{:S(2)}) copy-start(bf16[2048,128]{1,0:T(8,128)(2,1)} %own_ref.1) | copy-start | bytes 1572868
  0.0 14.0 %copy-start.2 = (s32[256,8]{0,1:T(8,128)S(1)}, s32[256,8]{0,1:T(8,128)}, u32[]{:S(2)}) copy-start(s32[256,8]{0,1:T(8,128)} %param.19) | copy-start | bytes 24580
  4.3 34.2 %copy-start.1 = (bf16[256,128]{1,0:T(8,128)(2,1)S(1)}, bf16[256,128]{1,0:T(8,128)(2,1)}, u32[]{:S(2)}) copy-start(bf16[256,128]{1,0:T(8,128)(2,1)} %residual_ref.1) | copy-start | bytes 196612
  4.3 39.4 %copy-start.3 = (f32[256,8]{0,1:T(8,128)S(1)}, f32[256,8]{0,1:T(8,128)}, u32[]{:S(2)}) copy-start(f32[256,8]{0,1:T(8,128)} %param.20) | copy-start | bytes 24580
  4.3 21.2 %collective-permute-start = (bf16[2048,128]{1,0:T(8,128)(2,1)S(1)}, bf16[2048,128]{1,0:T(8,128)(2,1)S(1)}, u32[]{:S(2)}, u32[]{:S(2)}) collective-permute-start(bf16[2048,128]{1,0:T(8,128)(2,1)S(1)} %copy-done), channel_id=1, source_target_pairs={{0,4},{4,0},{1,5},{5,1},{2,6},{6,2},{3,7},{7,3},{8,12},{12,8},{9,1... | collective-permute-start | bytes 1572872 | tf_op jit(solution)/shard_map/ppermute | solution.py:518
  6.1 19.5 %all-to-all-start = ((bf16[16,8,2176]{2,1,0:T(8,128)(2,1)}), bf16[16,8,2176]{2,1,0:T(8,128)(2,1)S(1)}, u32[]{:S(2)}, u32[]{:S(2)}) async-start(bf16[16,8,2176]{2,1,0:T(8,128)(2,1)} %attend.1), calls=%async_computation | async-start | bytes 1114112 | tf_op jit(solution)/shard_map/all_to_all | solution.py:389
  26.7 11.8 %all-to-all-start.1 = ((bf16[8,128,128]{2,1,0:T(8,128)(2,1)}), bf16[8,128,128]{2,1,0:T(8,128)(2,1)S(1)}, u32[]{:S(2)}, u32[]{:S(2)}) async-start(bf16[8,128,128]{2,1,0:T(8,128)(2,1)} %project.1), calls=%async_computation.1 | async-start | bytes 524288 | tf_op jit(solution)/shard_map/all_to_all | solution.py:389
  31.1 8.7 %collective-permute-start.1 = (f32[16,128]{1,0:T(8,128)S(1)}, f32[16,128]{1,0:T(8,128)S(1)}, u32[]{:S(2)}, u32[]{:S(2)}) collective-permute-start(f32[16,128]{1,0:T(8,128)S(1)} %convert_reduce_fusion), channel_id=1, source_target_pairs={{0,4},{4,0},{1,5},{5,1},{2,6},{6,2},{3,7},{7,3},{8,12},{12,8},{9,1... | collective-permute-start | bytes 24584 | tf_op jit(solution)/shard_map/ppermute | solution.py:522
  39.7 15.2 %all-to-all-start.2 = ((bf16[32,64,128]{2,1,0:T(8,128)(2,1)}), bf16[32,64,128]{2,1,0:T(8,128)(2,1)S(1)}, u32[]{:S(2)}, u32[]{:S(2)}) async-start(bf16[32,64,128]{2,1,0:T(8,128)(2,1)} %get-tuple-element.21), calls=%async_computation.2 | async-start | bytes 1048576 | tf_op jit(solution)/shard_map/all_to_all | solution.py:389
  54.9 4.7 %collective-permute-start.2 = (bf16[32,64,128]{2,1,0:T(8,128)(2,1)S(1)}, bf16[32,64,128]{2,1,0:T(8,128)(2,1)S(1)}, u32[]{:S(2)}, u32[]{:S(2)}) collective-permute-start(bf16[32,64,128]{2,1,0:T(8,128)(2,1)S(1)} %all-to-all-done.2.rows_ref), channel_id=1, source_target_pairs={{0,32},{32,0},{1,33},{33,1},{2,34},{34,2},{3,35},{35,3},{4,36},{36... | collective-permute-start | bytes 1572872 | tf_op jit(solution)/shard_map/ppermute | solution.py:535
  59.0 4.0 %collective-permute-start.3 = (bf16[64,4096]{1,0:T(8,128)(2,1)S(1)}, bf16[64,4096]{1,0:T(8,128)(2,1)S(1)}, u32[]{:S(2)}, u32[]{:S(2)}) collective-permute-start(bf16[64,4096]{1,0:T(8,128)(2,1)S(1)} %get-tuple-element.27), channel_id=1, source_target_pairs={{0,32},{32,0},{1,33},{33,1},{2,34},{34,2},{3,35},{35,3},{4,36},{36... | collective-permute-start | bytes 1572872 | tf_op jit(solution)/shard_map/ppermute | solution.py:565
  64.6 16.0 %all-to-all-start.3 = ((bf16[32,64,128]{2,1,0:T(8,128)(2,1)}), bf16[32,64,128]{2,1,0:T(8,128)(2,1)S(1)}, u32[]{:S(2)}, u32[]{:S(2)}) async-start(bf16[32,64,128]{2,1,0:T(8,128)(2,1)} %other_down.1), calls=%async_computation.3 | async-start | bytes 1048576 | tf_op jit(solution)/shard_map/all_to_all | solution.py:389
  81.3 1.4 %collective-permute-start.4 = (f32[256,128]{1,0:T(8,128)S(1)}, f32[256,128]{1,0:T(8,128)S(1)}, u32[]{:S(2)}, u32[]{:S(2)}) collective-permute-start(f32[256,128]{1,0:T(8,128)S(1)} %fusion.1), channel_id=1, source_target_pairs={{0,32},{32,0},{1,33},{33,1},{2,34},{34,2},{3,35},{35,3},{4,36},{36... | collective-permute-start | bytes 393224 | tf_op jit(solution)/shard_map/ppermute | solution.py:479
  82.7 5.8 %collective-permute-start.5 = (bf16[256,128]{1,0:T(8,128)(2,1)S(1)}, bf16[256,128]{1,0:T(8,128)(2,1)S(1)}, u32[]{:S(2)}, u32[]{:S(2)}) collective-permute-start(bf16[256,128]{1,0:T(8,128)(2,1)S(1)} %add_convert_fusion.1), channel_id=1, source_target_pairs={{0,64},{64,0},{1,65},{65,1},{2,66},{66,2},{3,67},{67,3},{4,68},{68... | collective-permute-start | bytes 196616 | tf_op jit(solution)/shard_map/ppermute | solution.py:481

commit v5 on v4

--- a/solution.py
+++ b/solution.py
@@ -52,12 +52,15 @@
     heads = queries_ref.shape[1] // HEAD_SIZE
     slots = keys.shape[1]
     scale = 1.0 / math.sqrt(HEAD_SIZE)
+    groups = rows // ROW_GROUP
+    spans = [pl.ds(g * ROW_GROUP, ROW_GROUP) for g in range(groups)]
     key_copies = [
-        pltpu.make_async_copy(cache_ref.at[0, r], keys.at[r], key_sems.at[r]) for r in range(rows)
+        pltpu.make_async_copy(cache_ref.at[0, span], keys.at[span], key_sems.at[g])
+        for g, span in enumerate(spans)
     ]
     value_copies = [
-        pltpu.make_async_copy(cache_ref.at[1, r], values.at[r], value_sems.at[r])
-        for r in range(rows)
+        pltpu.make_async_copy(cache_ref.at[1, span], values.at[span], value_sems.at[g])
+        for g, span in enumerate(spans)
     ]
     small_copies = [
         pltpu.make_async_copy(source, target, small_sems.at[i])
@@ -121,15 +124,12 @@
         ) / normalizer
 
     scored, weighed = {}, {}
-    groups = rows // ROW_GROUP
     members = lambda g: range(g * ROW_GROUP, (g + 1) * ROW_GROUP)
     for g in range(groups + 2):
         if g < groups:
-            for r in members(g):
-                key_copies[r].wait()
+            key_copies[g].wait()
         if g >= 2:
-            for r in members(g - 2):
-                value_copies[r].wait()
+            value_copies[g - 2].wait()
         if g < groups:
             for r in members(g):
                 scored[r] = score(r)

time: 89.8 us -> 89.5 us (level)
  no operation moved by 1% of the time
where the time goes in v5:
time: 89.5 us; the launch traced here: 89 us
  waiting for transfers between devices  43.4 us (48%)
  starting transfers between devices  26.1 us (29%)
  Pallas kernels  17 us (19%)
  other arithmetic  0.98 us (1%)
  matrix products  0.98 us (1%)
    all_to_all x4, waiting for transfers between devices, exchange(): return lax.all_to_all(blocks, axes, 0, 0, tiled=True)  37.6 us
    all_to_all x4, starting transfers between devices, exchange(): return lax.all_to_all(blocks, axes, 0, 0, tiled=True)  20.2 us
    pallas_call x3, Pallas kernels, expert_call(): pl.pallas_call(kernel, out_shape=[space(shape, jnp.bfloat16) for space, s...  8.99 us
    ppermute x1, waiting for transfers between devices, sum_over_sec(): lax.ppermute(pair, 'y_hi', SWAP).astype(jnp.float32)  4.39 us
    pallas_call x1, Pallas kernels, attend(): pl.pallas_call(attend_kernel, out_shape=jax.ShapeDtypeStruct((PLANE, rows...  4.04 us
    ppermute x1, starting transfers between devices, shards(): pair_gain = lax.ppermute(own_gain, 'y_lo', SWAP)  2.1 us
  transfers between devices with their start and end apart: 10, of which 6 were waited for; matrix products, arithmetic and copies ran while one was open for 1% of the time, Pallas kernels for 12%

profile of v5, /device:TPU:0, one launch (start us, length us, event | category | flops | bytes accessed | tf_op | source)
XLA Modules:
  0.0 89.0 jit_solution(10390318601499490852)
XLA Ops:
  0.0 4.0 %attend.1 = bf16[16,8,2176]{2,1,0:T(8,128)(2,1)} custom-call(s32[8]{0:T(128)} %lengths_hbm.1, bf16[8,2048]{1,0:T(8,128)(2,1)} %queries_hbm.1, bf16[2,8,128]{2,1,0:T(8,128)(2,1)} %fresh_hbm.1, f32[1,128]{1,0:T(1,128)} %bitcast.28, bf16[2,8,1024,128]{3,2,1,0:T(8,128)(2,1)} %cache_ref.1), custom_call_target="tpu_custom_call" | custom-call | flops 67108864 | bytes 5242880 | tf_op jit(solution)/shard_map/attend/pallas_call | solution.py:161
  4.1 1.7 %collective-permute-start = (bf16[2048,128]{1,0:T(8,128)(2,1)S(1)}, bf16[2048,128]{1,0:T(8,128)(2,1)S(1)}, u32[]{:S(2)}, u32[]{:S(2)}) collective-permute-start(bf16[2048,128]{1,0:T(8,128)(2,1)S(1)} %copy-done), channel_id=1, source_target_pairs={{0,4},{4,0},{1,5},{5,1},{2,6},{6,2},{3,7},{7,3},{8,12},{12,8},{9,1... | collective-permute-start | bytes 1572872 | tf_op jit(solution)/shard_map/ppermute | solution.py:518
  5.8 7.9 %all-to-all-start = ((bf16[16,8,2176]{2,1,0:T(8,128)(2,1)}), bf16[16,8,2176]{2,1,0:T(8,128)(2,1)S(1)}, u32[]{:S(2)}, u32[]{:S(2)}) async-start(bf16[16,8,2176]{2,1,0:T(8,128)(2,1)} %attend.1), calls=%async_computation | async-start | bytes 1114112 | tf_op jit(solution)/shard_map/all_to_all | solution.py:389
  13.8 0.3 fusion.2
  14.1 11.2 %all-to-all-done.gathered_ref = bf16[16,8,2176]{2,1,0:T(8,128)(2,1)S(1)} async-done(((bf16[16,8,2176]{2,1,0:T(8,128)(2,1)}), bf16[16,8,2176]{2,1,0:T(8,128)(2,1)S(1)}, u32[]{:S(2)}, u32[]{:S(2)}) %all-to-all-start) | async-done | bytes 557088 | tf_op jit(solution)/shard_map/all_to_all | solution.py:389
  25.3 1.1 %project.1 = bf16[8,128,128]{2,1,0:T(8,128)(2,1)} custom-call(bf16[16,8,2176]{2,1,0:T(8,128)(2,1)S(1)} %all-to-all-done.gathered_ref, bf16[2048,128]{1,0:T(8,128)(2,1)S(1)} %copy-done, bf16[2048,128]{1,0:T(8,128)(2,1)S(1)} %collective-permute-done.pair_ref), custom_call_target="tpu_custom_call" | custom-call | flops 134217728 | bytes 2097152 | tf_op jit(solution)/shard_map/project/pallas_call | solution.py:407
  26.5 4.2 %all-to-all-start.1 = ((bf16[8,128,128]{2,1,0:T(8,128)(2,1)}), bf16[8,128,128]{2,1,0:T(8,128)(2,1)S(1)}, u32[]{:S(2)}, u32[]{:S(2)}) async-start(bf16[8,128,128]{2,1,0:T(8,128)(2,1)} %project.1), calls=%async_computation.1 | async-start | bytes 524288 | tf_op jit(solution)/shard_map/all_to_all | solution.py:389
  30.8 2.1 %collective-permute-start.1 = (f32[16,128]{1,0:T(8,128)S(1)}, f32[16,128]{1,0:T(8,128)S(1)}, u32[]{:S(2)}, u32[]{:S(2)}) collective-permute-start(f32[16,128]{1,0:T(8,128)S(1)} %convert_reduce_fusion), channel_id=1, source_target_pairs={{0,4},{4,0},{1,5},{5,1},{2,6},{6,2},{3,7},{7,3},{8,12},{12,8},{9,1... | collective-permute-start | bytes 24584 | tf_op jit(solution)/shard_map/ppermute | solution.py:522
  32.9 5.4 %all-to-all-done.1.parts_ref = bf16[8,128,128]{2,1,0:T(8,128)(2,1)S(1)} async-done(((bf16[8,128,128]{2,1,0:T(8,128)(2,1)}), bf16[8,128,128]{2,1,0:T(8,128)(2,1)S(1)}, u32[]{:S(2)}, u32[]{:S(2)}) %all-to-all-start.1) | async-done | bytes 262176 | tf_op jit(solution)/shard_map/all_to_all | solution.py:389
  38.3 1.2 %dispatch.1 = (f32[256,128]{1,0:T(8,128)S(1)}, bf16[32,64,128]{2,1,0:T(8,128)(2,1)}) custom-call(bf16[8,128,128]{2,1,0:T(8,128)(2,1)S(1)} %all-to-all-done.1.parts_ref, bf16[256,128]{1,0:T(8,128)(2,1)S(1)} %copy-done.1, s32[32,256]{1,0:T(8,128)S(1)} %bitcast.23), custom_call_target="tpu_custom_call" | custom-call | flops 134217728 | bytes 2097152 | tf_op jit(solution)/shard_map/dispatch/pallas_call | solution.py:457
  39.5 3.9 %all-to-all-start.2 = ((bf16[32,64,128]{2,1,0:T(8,128)(2,1)}), bf16[32,64,128]{2,1,0:T(8,128)(2,1)S(1)}, u32[]{:S(2)}, u32[]{:S(2)}) async-start(bf16[32,64,128]{2,1,0:T(8,128)(2,1)} %get-tuple-element.21), calls=%async_computation.2 | async-start | bytes 1048576 | tf_op jit(solution)/shard_map/all_to_all | solution.py:389
  43.7 1.7 %preload.1 = (bf16[1536,384]{1,0:T(8,128)(2,1)S(1)}, bf16[1536,384]{1,0:T(8,128)(2,1)S(1)}) custom-call(bf16[2,4096,384]{2,1,0:T(8,128)(2,1)} %gate_hbm.4, bf16[2,4096,384]{2,1,0:T(8,128)(2,1)} %up_hbm.4), custom_call_target="tpu_custom_call" | custom-call | bytes 4718592 | tf_op jit(solution)/shard_map/preload/pallas_call | solution.py:279
  45.4 9.3 %all-to-all-done.2.rows_ref = bf16[32,64,128]{2,1,0:T(8,128)(2,1)S(1)} async-done(((bf16[32,64,128]{2,1,0:T(8,128)(2,1)}), bf16[32,64,128]{2,1,0:T(8,128)(2,1)S(1)}, u32[]{:S(2)}, u32[]{:S(2)}) %all-to-all-start.2) | async-done | bytes 524320 | tf_op jit(solution)/shard_map/all_to_all | solution.py:389
  54.7 4.1 %own_expert.1 = (bf16[64,4096]{1,0:T(8,128)(2,1)S(1)}, bf16[4,384,1024]{2,1,0:T(8,128)(2,1)S(1)}) custom-call(bf16[32,64,128]{2,1,0:T(8,128)(2,1)S(1)} %all-to-all-done.2.rows_ref, f32[32,128]{1,0:T(8,128)S(1)} %bitcast.21, f32[2,64,1]{2,1,0:T(8,128)S(1)} %copy.20.share_ref, bf16[1536,384]{1,0:T(8,128)(2,1)S(1)} %get-tuple-element.25.first_gate, ...), custom_call_target="tpu_custom_call" | custom-call | flops 603979776 | bytes 9437184 | tf_op jit(solution)/shard_map/own_expert/pallas_call | solution.py:370
  58.8 0.6 collective-permute-start.3
  59.4 3.4 %other_gate.1.activation_ref = bf16[64,384]{1,0:T(8,128)(2,1)S(1)} custom-call(bf16[32,64,128]{2,1,0:T(8,128)(2,1)S(1)} %collective-permute-done.2.rows_ref, f32[32,128]{1,0:T(8,128)S(1)} %bitcast.22, bf16[2,4096,384]{2,1,0:T(8,128)(2,1)} %gate_hbm.4, bf16[2,4096,384]{2,1,0:T(8,128)(2,1)} %up_hbm.4), custom_call_target="tpu_custom_call" | custom-call | flops 402653184 | bytes 6291456 | tf_op jit(solution)/shard_map/other_gate/pallas_call | solution.py:370
  62.8 1.5 %other_down.1 = bf16[32,64,128]{2,1,0:T(8,128)(2,1)} custom-call(bf16[64,384]{1,0:T(8,128)(2,1)S(1)} %other_gate.1.activation_ref, bf16[64,4096]{1,0:T(8,128)(2,1)S(1)} %collective-permute-done.3.moved_ref, f32[2,64,1]{2,1,0:T(8,128)S(1)} %copy.20.share_ref, bf16[4,384,1024]{2,1,0:T(8,128)(2,1)S(1)} %get-tuple-element.28.down), custom_call_target="tpu_custom_call" | custom-call | tf_op jit(solution)/shard_map/other_down/pallas_call | solution.py:370
  64.3 4.2 %all-to-all-start.3 = ((bf16[32,64,128]{2,1,0:T(8,128)(2,1)}), bf16[32,64,128]{2,1,0:T(8,128)(2,1)S(1)}, u32[]{:S(2)}, u32[]{:S(2)}) async-start(bf16[32,64,128]{2,1,0:T(8,128)(2,1)} %other_down.1), calls=%async_computation.3 | async-start | bytes 1048576 | tf_op jit(solution)/shard_map/all_to_all | solution.py:389
  68.5 11.8 %all-to-all-done.3 = bf16[32,64,128]{2,1,0:T(8,128)(2,1)S(1)} async-done(((bf16[32,64,128]{2,1,0:T(8,128)(2,1)}), bf16[32,64,128]{2,1,0:T(8,128)(2,1)S(1)}, u32[]{:S(2)}, u32[]{:S(2)}) %all-to-all-start.3) | async-done | bytes 524320 | tf_op jit(solution)/shard_map/all_to_all | solution.py:389
  80.3 0.7 fusion.1
  81.1 1.3 %collective-permute-done.4 = f32[256,128]{1,0:T(8,128)S(1)} collective-permute-done((f32[256,128]{1,0:T(8,128)S(1)}, f32[256,128]{1,0:T(8,128)S(1)}, u32[]{:S(2)}, u32[]{:S(2)}) %collective-permute-start.4) | collective-permute-done | bytes 131104 | tf_op jit(solution)/shard_map/ppermute | solution.py:479
  82.5 1.5 %collective-permute-start.5 = (bf16[256,128]{1,0:T(8,128)(2,1)S(1)}, bf16[256,128]{1,0:T(8,128)(2,1)S(1)}, u32[]{:S(2)}, u32[]{:S(2)}) collective-permute-start(bf16[256,128]{1,0:T(8,128)(2,1)S(1)} %add_convert_fusion.1), channel_id=1, source_target_pairs={{0,64},{64,0},{1,65},{65,1},{2,66},{66,2},{3,67},{67,3},{4,68},{68... | collective-permute-start | bytes 196616 | tf_op jit(solution)/shard_map/ppermute | solution.py:481
  83.9 4.4 %collective-permute-done.5 = bf16[256,128]{1,0:T(8,128)(2,1)S(1)} collective-permute-done((bf16[256,128]{1,0:T(8,128)(2,1)S(1)}, bf16[256,128]{1,0:T(8,128)(2,1)S(1)}, u32[]{:S(2)}, u32[]{:S(2)}) %collective-permute-start.5) | collective-permute-done | bytes 65568 | tf_op jit(solution)/shard_map/ppermute | solution.py:481
  88.3 0.7 add_convert_fusion
  (28 shorter events, 0.7 us)
Async XLA Ops:
  0.0 4.1 %copy-start = (bf16[2048,128]{1,0:T(8,128)(2,1)S(1)}, bf16[2048,128]{1,0:T(8,128)(2,1)}, u32[]{:S(2)}) copy-start(bf16[2048,128]{1,0:T(8,128)(2,1)} %own_ref.1) | copy-start | bytes 1572868
  0.0 13.7 %copy-start.2 = (s32[256,8]{0,1:T(8,128)S(1)}, s32[256,8]{0,1:T(8,128)}, u32[]{:S(2)}) copy-start(s32[256,8]{0,1:T(8,128)} %param.19) | copy-start | bytes 24580
  4.1 34.2 %copy-start.1 = (bf16[256,128]{1,0:T(8,128)(2,1)S(1)}, bf16[256,128]{1,0:T(8,128)(2,1)}, u32[]{:S(2)}) copy-start(bf16[256,128]{1,0:T(8,128)(2,1)} %residual_ref.1) | copy-start | bytes 196612
  4.1 39.4 %copy-start.3 = (f32[256,8]{0,1:T(8,128)S(1)}, f32[256,8]{0,1:T(8,128)}, u32[]{:S(2)}) copy-start(f32[256,8]{0,1:T(8,128)} %param.20) | copy-start | bytes 24580
  4.1 21.2 %collective-permute-start = (bf16[2048,128]{1,0:T(8,128)(2,1)S(1)}, bf16[2048,128]{1,0:T(8,128)(2,1)S(1)}, u32[]{:S(2)}, u32[]{:S(2)}) collective-permute-start(bf16[2048,128]{1,0:T(8,128)(2,1)S(1)} %copy-done), channel_id=1, source_target_pairs={{0,4},{4,0},{1,5},{5,1},{2,6},{6,2},{3,7},{7,3},{8,12},{12,8},{9,1... | collective-permute-start | bytes 1572872 | tf_op jit(solution)/shard_map/ppermute | solution.py:518
  5.8 19.5 %all-to-all-start = ((bf16[16,8,2176]{2,1,0:T(8,128)(2,1)}), bf16[16,8,2176]{2,1,0:T(8,128)(2,1)S(1)}, u32[]{:S(2)}, u32[]{:S(2)}) async-start(bf16[16,8,2176]{2,1,0:T(8,128)(2,1)} %attend.1), calls=%async_computation | async-start | bytes 1114112 | tf_op jit(solution)/shard_map/all_to_all | solution.py:389
  26.5 11.8 %all-to-all-start.1 = ((bf16[8,128,128]{2,1,0:T(8,128)(2,1)}), bf16[8,128,128]{2,1,0:T(8,128)(2,1)S(1)}, u32[]{:S(2)}, u32[]{:S(2)}) async-start(bf16[8,128,128]{2,1,0:T(8,128)(2,1)} %project.1), calls=%async_computation.1 | async-start | bytes 524288 | tf_op jit(solution)/shard_map/all_to_all | solution.py:389
  30.8 8.7 %collective-permute-start.1 = (f32[16,128]{1,0:T(8,128)S(1)}, f32[16,128]{1,0:T(8,128)S(1)}, u32[]{:S(2)}, u32[]{:S(2)}) collective-permute-start(f32[16,128]{1,0:T(8,128)S(1)} %convert_reduce_fusion), channel_id=1, source_target_pairs={{0,4},{4,0},{1,5},{5,1},{2,6},{6,2},{3,7},{7,3},{8,12},{12,8},{9,1... | collective-permute-start | bytes 24584 | tf_op jit(solution)/shard_map/ppermute | solution.py:522
  39.5 15.2 %all-to-all-start.2 = ((bf16[32,64,128]{2,1,0:T(8,128)(2,1)}), bf16[32,64,128]{2,1,0:T(8,128)(2,1)S(1)}, u32[]{:S(2)}, u32[]{:S(2)}) async-start(bf16[32,64,128]{2,1,0:T(8,128)(2,1)} %get-tuple-element.21), calls=%async_computation.2 | async-start | bytes 1048576 | tf_op jit(solution)/shard_map/all_to_all | solution.py:389
  54.7 4.7 %collective-permute-start.2 = (bf16[32,64,128]{2,1,0:T(8,128)(2,1)S(1)}, bf16[32,64,128]{2,1,0:T(8,128)(2,1)S(1)}, u32[]{:S(2)}, u32[]{:S(2)}) collective-permute-start(bf16[32,64,128]{2,1,0:T(8,128)(2,1)S(1)} %all-to-all-done.2.rows_ref), channel_id=1, source_target_pairs={{0,32},{32,0},{1,33},{33,1},{2,34},{34,2},{3,35},{35,3},{4,36},{36... | collective-permute-start | bytes 1572872 | tf_op jit(solution)/shard_map/ppermute | solution.py:535
  58.8 4.0 %collective-permute-start.3 = (bf16[64,4096]{1,0:T(8,128)(2,1)S(1)}, bf16[64,4096]{1,0:T(8,128)(2,1)S(1)}, u32[]{:S(2)}, u32[]{:S(2)}) collective-permute-start(bf16[64,4096]{1,0:T(8,128)(2,1)S(1)} %get-tuple-element.27), channel_id=1, source_target_pairs={{0,32},{32,0},{1,33},{33,1},{2,34},{34,2},{3,35},{35,3},{4,36},{36... | collective-permute-start | bytes 1572872 | tf_op jit(solution)/shard_map/ppermute | solution.py:565
  64.3 16.0 %all-to-all-start.3 = ((bf16[32,64,128]{2,1,0:T(8,128)(2,1)}), bf16[32,64,128]{2,1,0:T(8,128)(2,1)S(1)}, u32[]{:S(2)}, u32[]{:S(2)}) async-start(bf16[32,64,128]{2,1,0:T(8,128)(2,1)} %other_down.1), calls=%async_computation.3 | async-start | bytes 1048576 | tf_op jit(solution)/shard_map/all_to_all | solution.py:389
  81.0 1.4 %collective-permute-start.4 = (f32[256,128]{1,0:T(8,128)S(1)}, f32[256,128]{1,0:T(8,128)S(1)}, u32[]{:S(2)}, u32[]{:S(2)}) collective-permute-start(f32[256,128]{1,0:T(8,128)S(1)} %fusion.1), channel_id=1, source_target_pairs={{0,32},{32,0},{1,33},{33,1},{2,34},{34,2},{3,35},{35,3},{4,36},{36... | collective-permute-start | bytes 393224 | tf_op jit(solution)/shard_map/ppermute | solution.py:479
  82.5 5.8 %collective-permute-start.5 = (bf16[256,128]{1,0:T(8,128)(2,1)S(1)}, bf16[256,128]{1,0:T(8,128)(2,1)S(1)}, u32[]{:S(2)}, u32[]{:S(2)}) collective-permute-start(bf16[256,128]{1,0:T(8,128)(2,1)S(1)} %add_convert_fusion.1), channel_id=1, source_target_pairs={{0,64},{64,0},{1,65},{65,1},{2,66},{66,2},{3,67},{67,3},{4,68},{68... | collective-permute-start | bytes 196616 | tf_op jit(solution)/shard_map/ppermute | solution.py:481

commit v6 on v5

--- a/solution.py
+++ b/solution.py
@@ -18,7 +18,7 @@
 PLANE = 16
 GATE_CHUNKS = 4
 FIRST = 1536
-DOWN_CHUNKS = 4
+DOWN_CHUNKS = 2
 ROW_GROUP = 4
 AXES = {"y_hi": 2, "core": 2, "z": 4, "y_lo": 2, "x": 4}
 SEC = ("y_hi", "core")
@@ -476,7 +476,8 @@
 
 
 def sum_over_sec(part):
-    pair = part + lax.ppermute(part, "core", SWAP)
+    half = part.astype(jnp.bfloat16)
+    pair = half.astype(jnp.float32) + lax.ppermute(half, "core", SWAP).astype(jnp.float32)
     pair = pair.astype(jnp.bfloat16)
     return pair.astype(jnp.float32) + lax.ppermute(pair, "y_hi", SWAP).astype(jnp.float32)
 

time: 89.5 us -> 89.5 us (level)
  no operation moved by 1% of the time
where the time goes in v6:
time: 89.5 us; the launch traced here: 89 us
  waiting for transfers between devices  43.3 us (48%)
  starting transfers between devices  26.1 us (29%)
  Pallas kernels  17.1 us (19%)
  matrix products  1.03 us (1%)
  other arithmetic  0.98 us (1%)
    all_to_all x4, waiting for transfers between devices, exchange(): return lax.all_to_all(blocks, axes, 0, 0, tiled=True)  37.6 us
    all_to_all x4, starting transfers between devices, exchange(): return lax.all_to_all(blocks, axes, 0, 0, tiled=True)  20.2 us
    pallas_call x3, Pallas kernels, expert_call(): pl.pallas_call(kernel, out_shape=[space(shape, jnp.bfloat16) for space, s...  9.08 us
    ppermute x1, waiting for transfers between devices, sum_over_sec(): lax.ppermute(pair, 'y_hi', SWAP).astype(jnp.float32)  4.39 us
    pallas_call x1, Pallas kernels, attend(): pl.pallas_call(attend_kernel, out_shape=jax.ShapeDtypeStruct((PLANE, rows...  4.04 us
    ppermute x1, starting transfers between devices, shards(): pair_gain = lax.ppermute(own_gain, 'y_lo', SWAP)  2.1 us
  transfers between devices with their start and end apart: 10, of which 6 were waited for; matrix products, arithmetic and copies ran while one was open for 1% of the time, Pallas kernels for 12%

profile of v6, /device:TPU:0, one launch (start us, length us, event | category | flops | bytes accessed | tf_op | source)
XLA Modules:
  0.0 89.0 jit_solution(10545133807724863593)
XLA Ops:
  0.0 4.0 %attend.1 = bf16[16,8,2176]{2,1,0:T(8,128)(2,1)} custom-call(s32[8]{0:T(128)} %lengths_hbm.1, bf16[8,2048]{1,0:T(8,128)(2,1)} %queries_hbm.1, bf16[2,8,128]{2,1,0:T(8,128)(2,1)} %fresh_hbm.1, f32[1,128]{1,0:T(1,128)} %bitcast.30, bf16[2,8,1024,128]{3,2,1,0:T(8,128)(2,1)} %cache_ref.1), custom_call_target="tpu_custom_call" | custom-call | flops 67108864 | bytes 5242880 | tf_op jit(solution)/shard_map/attend/pallas_call | solution.py:161
  4.1 1.7 %collective-permute-start = (bf16[2048,128]{1,0:T(8,128)(2,1)S(1)}, bf16[2048,128]{1,0:T(8,128)(2,1)S(1)}, u32[]{:S(2)}, u32[]{:S(2)}) collective-permute-start(bf16[2048,128]{1,0:T(8,128)(2,1)S(1)} %copy-done), channel_id=1, source_target_pairs={{0,4},{4,0},{1,5},{5,1},{2,6},{6,2},{3,7},{7,3},{8,12},{12,8},{9,1... | collective-permute-start | bytes 1572872 | tf_op jit(solution)/shard_map/ppermute | solution.py:519
  5.8 7.9 %all-to-all-start = ((bf16[16,8,2176]{2,1,0:T(8,128)(2,1)}), bf16[16,8,2176]{2,1,0:T(8,128)(2,1)S(1)}, u32[]{:S(2)}, u32[]{:S(2)}) async-start(bf16[16,8,2176]{2,1,0:T(8,128)(2,1)} %attend.1), calls=%async_computation | async-start | bytes 1114112 | tf_op jit(solution)/shard_map/all_to_all | solution.py:389
  13.8 0.3 fusion.3
  14.1 11.2 %all-to-all-done.gathered_ref = bf16[16,8,2176]{2,1,0:T(8,128)(2,1)S(1)} async-done(((bf16[16,8,2176]{2,1,0:T(8,128)(2,1)}), bf16[16,8,2176]{2,1,0:T(8,128)(2,1)S(1)}, u32[]{:S(2)}, u32[]{:S(2)}) %all-to-all-start) | async-done | bytes 557088 | tf_op jit(solution)/shard_map/all_to_all | solution.py:389
  25.3 1.1 %project.1 = bf16[8,128,128]{2,1,0:T(8,128)(2,1)} custom-call(bf16[16,8,2176]{2,1,0:T(8,128)(2,1)S(1)} %all-to-all-done.gathered_ref, bf16[2048,128]{1,0:T(8,128)(2,1)S(1)} %copy-done, bf16[2048,128]{1,0:T(8,128)(2,1)S(1)} %collective-permute-done.pair_ref), custom_call_target="tpu_custom_call" | custom-call | flops 134217728 | bytes 2097152 | tf_op jit(solution)/shard_map/project/pallas_call | solution.py:407
  26.5 4.2 %all-to-all-start.1 = ((bf16[8,128,128]{2,1,0:T(8,128)(2,1)}), bf16[8,128,128]{2,1,0:T(8,128)(2,1)S(1)}, u32[]{:S(2)}, u32[]{:S(2)}) async-start(bf16[8,128,128]{2,1,0:T(8,128)(2,1)} %project.1), calls=%async_computation.1 | async-start | bytes 524288 | tf_op jit(solution)/shard_map/all_to_all | solution.py:389
  30.8 2.1 %collective-permute-start.1 = (f32[16,128]{1,0:T(8,128)S(1)}, f32[16,128]{1,0:T(8,128)S(1)}, u32[]{:S(2)}, u32[]{:S(2)}) collective-permute-start(f32[16,128]{1,0:T(8,128)S(1)} %convert_reduce_fusion), channel_id=1, source_target_pairs={{0,4},{4,0},{1,5},{5,1},{2,6},{6,2},{3,7},{7,3},{8,12},{12,8},{9,1... | collective-permute-start | bytes 24584 | tf_op jit(solution)/shard_map/ppermute | solution.py:523
  32.9 5.4 %all-to-all-done.1.parts_ref = bf16[8,128,128]{2,1,0:T(8,128)(2,1)S(1)} async-done(((bf16[8,128,128]{2,1,0:T(8,128)(2,1)}), bf16[8,128,128]{2,1,0:T(8,128)(2,1)S(1)}, u32[]{:S(2)}, u32[]{:S(2)}) %all-to-all-start.1) | async-done | bytes 262176 | tf_op jit(solution)/shard_map/all_to_all | solution.py:389
  38.3 1.2 %dispatch.1 = (f32[256,128]{1,0:T(8,128)S(1)}, bf16[32,64,128]{2,1,0:T(8,128)(2,1)}) custom-call(bf16[8,128,128]{2,1,0:T(8,128)(2,1)S(1)} %all-to-all-done.1.parts_ref, bf16[256,128]{1,0:T(8,128)(2,1)S(1)} %copy-done.1, s32[32,256]{1,0:T(8,128)S(1)} %bitcast.25), custom_call_target="tpu_custom_call" | custom-call | flops 134217728 | bytes 2097152 | tf_op jit(solution)/shard_map/dispatch/pallas_call | solution.py:457
  39.5 3.9 %all-to-all-start.2 = ((bf16[32,64,128]{2,1,0:T(8,128)(2,1)}), bf16[32,64,128]{2,1,0:T(8,128)(2,1)S(1)}, u32[]{:S(2)}, u32[]{:S(2)}) async-start(bf16[32,64,128]{2,1,0:T(8,128)(2,1)} %get-tuple-element.21), calls=%async_computation.2 | async-start | bytes 1048576 | tf_op jit(solution)/shard_map/all_to_all | solution.py:389
  43.7 1.7 %preload.1 = (bf16[1536,384]{1,0:T(8,128)(2,1)S(1)}, bf16[1536,384]{1,0:T(8,128)(2,1)S(1)}) custom-call(bf16[2,4096,384]{2,1,0:T(8,128)(2,1)} %gate_hbm.4, bf16[2,4096,384]{2,1,0:T(8,128)(2,1)} %up_hbm.4), custom_call_target="tpu_custom_call" | custom-call | bytes 4718592 | tf_op jit(solution)/shard_map/preload/pallas_call | solution.py:279
  45.4 9.3 %all-to-all-done.2.rows_ref = bf16[32,64,128]{2,1,0:T(8,128)(2,1)S(1)} async-done(((bf16[32,64,128]{2,1,0:T(8,128)(2,1)}), bf16[32,64,128]{2,1,0:T(8,128)(2,1)S(1)}, u32[]{:S(2)}, u32[]{:S(2)}) %all-to-all-start.2) | async-done | bytes 524320 | tf_op jit(solution)/shard_map/all_to_all | solution.py:389
  54.7 4.1 %own_expert.1 = (bf16[64,4096]{1,0:T(8,128)(2,1)S(1)}, bf16[2,384,2048]{2,1,0:T(8,128)(2,1)S(1)}) custom-call(bf16[32,64,128]{2,1,0:T(8,128)(2,1)S(1)} %all-to-all-done.2.rows_ref, f32[32,128]{1,0:T(8,128)S(1)} %bitcast.23, f32[2,64,1]{2,1,0:T(8,128)S(1)} %copy.20.share_ref, bf16[1536,384]{1,0:T(8,128)(2,1)S(1)} %get-tuple-element.25.first_gate, ...), custom_call_target="tpu_custom_call" | custom-call | flops 603979776 | bytes 9437184 | tf_op jit(solution)/shard_map/own_expert/pallas_call | solution.py:370
  58.8 0.6 collective-permute-start.3
  59.4 3.4 %other_gate.1.activation_ref = bf16[64,384]{1,0:T(8,128)(2,1)S(1)} custom-call(bf16[32,64,128]{2,1,0:T(8,128)(2,1)S(1)} %collective-permute-done.2.rows_ref, f32[32,128]{1,0:T(8,128)S(1)} %bitcast.24, bf16[2,4096,384]{2,1,0:T(8,128)(2,1)} %gate_hbm.4, bf16[2,4096,384]{2,1,0:T(8,128)(2,1)} %up_hbm.4), custom_call_target="tpu_custom_call" | custom-call | flops 402653184 | bytes 6291456 | tf_op jit(solution)/shard_map/other_gate/pallas_call | solution.py:370
  62.8 1.5 %other_down.1 = bf16[32,64,128]{2,1,0:T(8,128)(2,1)} custom-call(bf16[64,384]{1,0:T(8,128)(2,1)S(1)} %other_gate.1.activation_ref, bf16[64,4096]{1,0:T(8,128)(2,1)S(1)} %collective-permute-done.3.moved_ref, f32[2,64,1]{2,1,0:T(8,128)S(1)} %copy.20.share_ref, bf16[2,384,2048]{2,1,0:T(8,128)(2,1)S(1)} %get-tuple-element.28.down), custom_call_target="tpu_custom_call" | custom-call | tf_op jit(solution)/shard_map/other_down/pallas_call | solution.py:370
  64.4 4.2 %all-to-all-start.3 = ((bf16[32,64,128]{2,1,0:T(8,128)(2,1)}), bf16[32,64,128]{2,1,0:T(8,128)(2,1)S(1)}, u32[]{:S(2)}, u32[]{:S(2)}) async-start(bf16[32,64,128]{2,1,0:T(8,128)(2,1)} %other_down.1), calls=%async_computation.3 | async-start | bytes 1048576 | tf_op jit(solution)/shard_map/all_to_all | solution.py:389
  68.6 11.8 %all-to-all-done.3 = bf16[32,64,128]{2,1,0:T(8,128)(2,1)S(1)} async-done(((bf16[32,64,128]{2,1,0:T(8,128)(2,1)}), bf16[32,64,128]{2,1,0:T(8,128)(2,1)S(1)}, u32[]{:S(2)}, u32[]{:S(2)}) %all-to-all-start.3) | async-done | bytes 524320 | tf_op jit(solution)/shard_map/all_to_all | solution.py:389
  80.4 0.8 fusion.2
  81.2 1.2 %collective-permute-done.4 = bf16[256,128]{1,0:T(8,128)(2,1)S(1)} collective-permute-done((bf16[256,128]{1,0:T(8,128)(2,1)S(1)}, bf16[256,128]{1,0:T(8,128)(2,1)S(1)}, u32[]{:S(2)}, u32[]{:S(2)}) %collective-permute-start.4) | collective-permute-done | bytes 65568 | tf_op jit(solution)/shard_map/ppermute | solution.py:480
  82.5 1.5 %collective-permute-start.5 = (bf16[256,128]{1,0:T(8,128)(2,1)S(1)}, bf16[256,128]{1,0:T(8,128)(2,1)S(1)}, u32[]{:S(2)}, u32[]{:S(2)}) collective-permute-start(bf16[256,128]{1,0:T(8,128)(2,1)S(1)} %add_convert_fusion.1), channel_id=1, source_target_pairs={{0,64},{64,0},{1,65},{65,1},{2,66},{66,2},{3,67},{67,3},{4,68},{68... | collective-permute-start | bytes 196616 | tf_op jit(solution)/shard_map/ppermute | solution.py:482
  84.0 4.4 %collective-permute-done.5 = bf16[256,128]{1,0:T(8,128)(2,1)S(1)} collective-permute-done((bf16[256,128]{1,0:T(8,128)(2,1)S(1)}, bf16[256,128]{1,0:T(8,128)(2,1)S(1)}, u32[]{:S(2)}, u32[]{:S(2)}) %collective-permute-start.5) | collective-permute-done | bytes 65568 | tf_op jit(solution)/shard_map/ppermute | solution.py:482
  88.4 0.7 add_convert_fusion
  (28 shorter events, 0.7 us)
Async XLA Ops:
  0.0 4.1 %copy-start = (bf16[2048,128]{1,0:T(8,128)(2,1)S(1)}, bf16[2048,128]{1,0:T(8,128)(2,1)}, u32[]{:S(2)}) copy-start(bf16[2048,128]{1,0:T(8,128)(2,1)} %own_ref.1) | copy-start | bytes 1572868
  0.0 13.7 %copy-start.2 = (s32[256,8]{0,1:T(8,128)S(1)}, s32[256,8]{0,1:T(8,128)}, u32[]{:S(2)}) copy-start(s32[256,8]{0,1:T(8,128)} %param.19) | copy-start | bytes 24580
  4.1 34.2 %copy-start.1 = (bf16[256,128]{1,0:T(8,128)(2,1)S(1)}, bf16[256,128]{1,0:T(8,128)(2,1)}, u32[]{:S(2)}) copy-start(bf16[256,128]{1,0:T(8,128)(2,1)} %residual_ref.1) | copy-start | bytes 196612
  4.1 39.4 %copy-start.3 = (f32[256,8]{0,1:T(8,128)S(1)}, f32[256,8]{0,1:T(8,128)}, u32[]{:S(2)}) copy-start(f32[256,8]{0,1:T(8,128)} %param.20) | copy-start | bytes 24580
  4.1 21.2 %collective-permute-start = (bf16[2048,128]{1,0:T(8,128)(2,1)S(1)}, bf16[2048,128]{1,0:T(8,128)(2,1)S(1)}, u32[]{:S(2)}, u32[]{:S(2)}) collective-permute-start(bf16[2048,128]{1,0:T(8,128)(2,1)S(1)} %copy-done), channel_id=1, source_target_pairs={{0,4},{4,0},{1,5},{5,1},{2,6},{6,2},{3,7},{7,3},{8,12},{12,8},{9,1... | collective-permute-start | bytes 1572872 | tf_op jit(solution)/shard_map/ppermute | solution.py:519
  5.8 19.5 %all-to-all-start = ((bf16[16,8,2176]{2,1,0:T(8,128)(2,1)}), bf16[16,8,2176]{2,1,0:T(8,128)(2,1)S(1)}, u32[]{:S(2)}, u32[]{:S(2)}) async-start(bf16[16,8,2176]{2,1,0:T(8,128)(2,1)} %attend.1), calls=%async_computation | async-start | bytes 1114112 | tf_op jit(solution)/shard_map/all_to_all | solution.py:389
  26.5 11.8 %all-to-all-start.1 = ((bf16[8,128,128]{2,1,0:T(8,128)(2,1)}), bf16[8,128,128]{2,1,0:T(8,128)(2,1)S(1)}, u32[]{:S(2)}, u32[]{:S(2)}) async-start(bf16[8,128,128]{2,1,0:T(8,128)(2,1)} %project.1), calls=%async_computation.1 | async-start | bytes 524288 | tf_op jit(solution)/shard_map/all_to_all | solution.py:389
  30.8 8.7 %collective-permute-start.1 = (f32[16,128]{1,0:T(8,128)S(1)}, f32[16,128]{1,0:T(8,128)S(1)}, u32[]{:S(2)}, u32[]{:S(2)}) collective-permute-start(f32[16,128]{1,0:T(8,128)S(1)} %convert_reduce_fusion), channel_id=1, source_target_pairs={{0,4},{4,0},{1,5},{5,1},{2,6},{6,2},{3,7},{7,3},{8,12},{12,8},{9,1... | collective-permute-start | bytes 24584 | tf_op jit(solution)/shard_map/ppermute | solution.py:523
  39.5 15.2 %all-to-all-start.2 = ((bf16[32,64,128]{2,1,0:T(8,128)(2,1)}), bf16[32,64,128]{2,1,0:T(8,128)(2,1)S(1)}, u32[]{:S(2)}, u32[]{:S(2)}) async-start(bf16[32,64,128]{2,1,0:T(8,128)(2,1)} %get-tuple-element.21), calls=%async_computation.2 | async-start | bytes 1048576 | tf_op jit(solution)/shard_map/all_to_all | solution.py:389
  54.7 4.7 %collective-permute-start.2 = (bf16[32,64,128]{2,1,0:T(8,128)(2,1)S(1)}, bf16[32,64,128]{2,1,0:T(8,128)(2,1)S(1)}, u32[]{:S(2)}, u32[]{:S(2)}) collective-permute-start(bf16[32,64,128]{2,1,0:T(8,128)(2,1)S(1)} %all-to-all-done.2.rows_ref), channel_id=1, source_target_pairs={{0,32},{32,0},{1,33},{33,1},{2,34},{34,2},{3,35},{35,3},{4,36},{36... | collective-permute-start | bytes 1572872 | tf_op jit(solution)/shard_map/ppermute | solution.py:536
  58.8 4.0 %collective-permute-start.3 = (bf16[64,4096]{1,0:T(8,128)(2,1)S(1)}, bf16[64,4096]{1,0:T(8,128)(2,1)S(1)}, u32[]{:S(2)}, u32[]{:S(2)}) collective-permute-start(bf16[64,4096]{1,0:T(8,128)(2,1)S(1)} %get-tuple-element.27), channel_id=1, source_target_pairs={{0,32},{32,0},{1,33},{33,1},{2,34},{34,2},{3,35},{35,3},{4,36},{36... | collective-permute-start | bytes 1572872 | tf_op jit(solution)/shard_map/ppermute | solution.py:566
  64.4 16.0 %all-to-all-start.3 = ((bf16[32,64,128]{2,1,0:T(8,128)(2,1)}), bf16[32,64,128]{2,1,0:T(8,128)(2,1)S(1)}, u32[]{:S(2)}, u32[]{:S(2)}) async-start(bf16[32,64,128]{2,1,0:T(8,128)(2,1)} %other_down.1), calls=%async_computation.3 | async-start | bytes 1048576 | tf_op jit(solution)/shard_map/all_to_all | solution.py:389
  81.2 1.3 %collective-permute-start.4 = (bf16[256,128]{1,0:T(8,128)(2,1)S(1)}, bf16[256,128]{1,0:T(8,128)(2,1)S(1)}, u32[]{:S(2)}, u32[]{:S(2)}) collective-permute-start(bf16[256,128]{1,0:T(8,128)(2,1)S(1)} %fusion.2), channel_id=1, source_target_pairs={{0,32},{32,0},{1,33},{33,1},{2,34},{34,2},{3,35},{35,3},{4,36},{36... | collective-permute-start | bytes 196616 | tf_op jit(solution)/shard_map/ppermute | solution.py:480
  82.5 5.8 %collective-permute-start.5 = (bf16[256,128]{1,0:T(8,128)(2,1)S(1)}, bf16[256,128]{1,0:T(8,128)(2,1)S(1)}, u32[]{:S(2)}, u32[]{:S(2)}) collective-permute-start(bf16[256,128]{1,0:T(8,128)(2,1)S(1)} %add_convert_fusion.1), channel_id=1, source_target_pairs={{0,64},{64,0},{1,65},{65,1},{2,66},{66,2},{3,67},{67,3},{4,68},{68... | collective-permute-start | bytes 196616 | tf_op jit(solution)/shard_map/ppermute | solution.py:482
